TPU v7x, 128 devices: a whole 4x4x4 slice. The times are simulated.
128 devices in a mesh: batch: 8 (over y, core), replica: 4 (over x), proto: 4 (over z).
Axes of the slice: x: 4, y: 4, z: 4, core: 2. Of those that a mesh axis runs over, the one named last changes fastest.
Arguments:
- view_one: bfloat16 [16384, 512], P(('batch', 'replica')), may hold values from -4 to 4
- view_two: bfloat16 [16384, 512], P(('batch', 'replica')), may hold values from -4 to 4
- prototypes: bfloat16 [16384, 512], P('proto'), may hold values from -8 to 8
- pairing: int32 [32, 512], P(('batch', 'replica')), may hold values from 0 to 511, as said below
Outputs:
- grad_one: float32 [16384, 512], P(('batch', 'replica'))
- grad_two: float32 [16384, 512], P(('batch', 'replica'))
- grad_prototypes: float32 [16384, 512], P('proto')
Inputs may be any that keep to these rules, and one draw needn't show every extreme that they name: Each row of pairing names every one of 0 to 511 once.
All inputs are finite; a program needn't handle non-finite values.
Results may differ from a plain program's by a relative error of at most 0.0018.
The roundings to bfloat16 on the way count: a program that leaves them out, or rounds other values in their place, can miss the bound.
Values sent between devices are 32-bit elements; how exact they have to be, the bound alone decides.
A program may use at most 128 MiB of HBM per device.

v0:
```python
import jax
import jax.numpy as jnp
from jax import lax
from jax.sharding import PartitionSpec as P

ITERS = 3


sink_eps = 0.05
softness_divisor = 0.1


def unit_rows(x):
    xf = x.astype(jnp.float32)
    inv = lax.rsqrt(jnp.sum(xf * xf, -1, keepdims=True) + 1e-06)
    return (xf * inv, inv)


def unit_back(grad, unit, inv):
    return inv * (grad - unit * jnp.sum(unit * grad, -1, keepdims=True))


def balance_single(similarity_logits):
    codes = jnp.exp(similarity_logits / sink_eps)
    for step in range(ITERS):
        codes = codes / lax.psum(jnp.sum(codes, 0, keepdims=True), ("batch", "replica"))
        codes = codes / lax.psum(jnp.sum(codes, 1, keepdims=True), "proto")
    return codes


def per_device(view_one, view_two, prototypes, pairing):
    unit_one, inv_one = unit_rows(view_one)
    unit_two, inv_two = unit_rows(view_two)
    unit_proto, inv_proto = unit_rows(prototypes)
    low_one = unit_one.astype(jnp.bfloat16)
    low_two = unit_two.astype(jnp.bfloat16)
    low_proto = unit_proto.astype(jnp.bfloat16)
    dims = (((1,), (1,)), ((), ()))
    logits_first_view = lax.dot_general(
        low_one, low_proto, dims, preferred_element_type=jnp.float32
    )
    logits_second_view = lax.dot_general(
        low_two, low_proto, dims, preferred_element_type=jnp.float32
    )
    codes_one = balance_single(logits_first_view)
    codes_two = balance_single(logits_second_view)
    exponent_first_view = jnp.exp(logits_first_view / softness_divisor)
    exponent_second_view = jnp.exp(logits_second_view / softness_divisor)
    total_one, total_two = lax.psum(
        (
            jnp.sum(exponent_first_view, 1, keepdims=True),
            jnp.sum(exponent_second_view, 1, keepdims=True),
        ),
        "proto",
    )
    local_rows = view_one.shape[0]
    partner = pairing[0]
    inverse = (
        jnp.zeros((local_rows,), jnp.int32).at[partner].set(jnp.arange(local_rows, dtype=jnp.int32))
    )
    target_one = codes_two[partner]
    target_two = codes_one[inverse]
    gradient_scale_factor = 0.5 / softness_divisor
    dscore_one = (gradient_scale_factor * (exponent_first_view / total_one - target_one)).astype(
        jnp.bfloat16
    )
    dscore_two = (gradient_scale_factor * (exponent_second_view / total_two - target_two)).astype(
        jnp.bfloat16
    )
    part_one = jnp.dot(dscore_one, low_proto, preferred_element_type=jnp.float32)
    part_two = jnp.dot(dscore_two, low_proto, preferred_element_type=jnp.float32)
    dunit_one, dunit_two = lax.psum((part_one, part_two), "proto")
    grad_one = unit_back(dunit_one, unit_one, inv_one)
    grad_two = unit_back(dunit_two, unit_two, inv_two)
    tdims = (((0,), (0,)), ((), ()))
    local_grad = lax.dot_general(dscore_one, low_one, tdims, preferred_element_type=jnp.float32)
    local_grad = local_grad + lax.dot_general(
        dscore_two, low_two, tdims, preferred_element_type=jnp.float32
    )
    dunit_proto = lax.psum(local_grad, ("batch", "replica"))
    grad_prototypes = unit_back(dunit_proto, unit_proto, inv_proto)
    return (grad_one, grad_two, grad_prototypes)


def solution(mesh):
    placed = (
        P(("batch", "replica"), None),
        P(("batch", "replica"), None),
        P("proto", None),
        P(("batch", "replica"), None),
    )
    return jax.shard_map(
        per_device,
        mesh=mesh,
        in_specs=placed,
        out_specs=(P(("batch", "replica"), None), P(("batch", "replica"), None), P("proto", None)),
        check_vma=False,
    )
```

profile of v0, /device:TPU:1, one launch (start us, length us, event | category | flops | bytes accessed | tf_op | source)
XLA Modules:
  0.0 741.3 jit_solution(12639128571758803586)
XLA Ops:
  7.2 0.0 all-reduce.12.cloned.1.call-start
  7.2 3.1 fusion.18
  10.3 1.2 fusion.46
  11.5 1.2 fusion.42
  12.8 0.0 copy-start
  12.8 0.0 copy-start.7
  12.8 8.5 %fusion.31 = (f32[4096]{0:T(1024)S(1)}, f32[512,4096]{1,0:T(8,128)}) fusion(bf16[4096,512]{1,0:T(8,128)(2,1)} %param.6, f32[4096]{0:T(1024)S(1)} %add_rsqrt_fusion, bf16[512,512]{1,0:T(8,128)(2,1)} %param.5, f32[512]{0:T(512)S(1)} %add_rsqrt_fusion.1), kind=kOutput, calls=%fused_computation.49 | convolution fusion | flops 2158751744 | bytes 13142016 | tf_op jit(solution)/shard_map/dot_general | solution.py:42
  21.3 0.0 copy-done
  21.3 0.0 copy-done.7
  21.3 5.0 fusion.32
  26.2 124.9 %all-reduce.2 = (f32[4096]{0:T(1024)S(1)}, f32[4096]{0:T(1024)S(1)}) all-reduce(f32[4096]{0:T(1024)S(1)} %get-tuple-element.25, f32[4096]{0:T(1024)S(1)} %get-tuple-element.27), channel_id=1, replica_groups=mesh['batch'=8,'replica'=4,'proto'=4] {'batch','replica'}, use_global_device_ids=true, to_apply=%region_6.0 | all-reduce | flops 8192 | bytes 65536 | tf_op jit(solution)/shard_map/psum | solution.py:26
  151.1 8.0 %fusion.30 = (f32[512]{0:T(512)S(1)}, f32[512]{0:T(512)S(1)}, f32[512]{0:T(512)S(1)}) fusion(f32[512,4096]{1,0:T(8,128)} %get-tuple-element.26, f32[4096]{0:T(1024)S(1)} %get-tuple-element.11, f32[4096]{0:T(1024)S(1)} %get-tuple-element.12, f32[512,4096]{1,0:T(8,128)} %get-tuple-element.28), kind=kLoop, calls=%fused_computation.47 | loop fusion | flops 16775680 | bytes 16816128 | tf_op jit(solution)/shard_map/reduce_sum | solution.py:52
  159.1 9.7 %all-reduce.5 = (f32[512]{0:T(512)S(1)}, f32[512]{0:T(512)S(1)}) all-reduce(f32[512]{0:T(512)S(1)} %get-tuple-element.4, f32[512]{0:T(512)S(1)} %get-tuple-element.29), channel_id=1, replica_groups=mesh['batch'=8,'replica'=4,'proto'=4] {'proto'}, use_global_device_ids=true, to_apply=%region_8.0 | all-reduce | flops 1024 | bytes 8192 | tf_op jit(solution)/shard_map/psum | solution.py:27
  168.9 4.7 fusion.22
  173.6 4.7 fusion.21
  178.2 126.6 %all-reduce.1 = (f32[4096]{0:T(1024)S(1)}, f32[4096]{0:T(1024)S(1)}) all-reduce(f32[4096]{0:T(1024)S(1)} %fusion.21, f32[4096]{0:T(1024)S(1)} %fusion.22), channel_id=1, replica_groups=mesh['batch'=8,'replica'=4,'proto'=4] {'batch','replica'}, use_global_device_ids=true, to_apply=%region_10.0 | all-reduce | flops 8192 | bytes 65536 | tf_op jit(solution)/shard_map/psum | solution.py:26
  304.8 4.7 fusion.23
  309.5 4.7 fusion.24
  314.2 6.0 all-reduce.4
  320.2 5.0 fusion.26
  325.2 5.0 fusion.25
  330.1 125.5 %all-reduce = (f32[4096]{0:T(1024)S(1)}, f32[4096]{0:T(1024)S(1)}) all-reduce(f32[4096]{0:T(1024)S(1)} %fusion.25, f32[4096]{0:T(1024)S(1)} %fusion.26), channel_id=1, replica_groups=mesh['batch'=8,'replica'=4,'proto'=4] {'batch','replica'}, use_global_device_ids=true, to_apply=%region_14.0 | all-reduce | flops 8192 | bytes 65536 | tf_op jit(solution)/shard_map/psum | solution.py:26
  455.7 6.4 fusion.27
  462.1 5.3 fusion.28
  467.4 7.8 %all-reduce.3 = (f32[512]{0:T(512)S(1)}, f32[512]{0:T(512)S(1)}, f32[512]{0:T(512)S(1)}, f32[512]{0:T(512)S(1)}) all-reduce(f32[512]{0:T(512)S(1)} %fusion.28, f32[512]{0:T(512)S(1)} %get-tuple-element.6, f32[512]{0:T(512)S(1)} %get-tuple-element.5, ...), channel_id=1, replica_groups=mesh['batch'=8,'replica'=4,'proto'=4] {'proto'}, use_global_device_ids=true, to_apply=%region_16.0 | all-reduce | flops 2048 | bytes 16384 | tf_op jit(solution)/shard_map/psum | solution.py:27
  475.3 0.0 copy-start.9
  475.3 7.4 fusion.19
  482.7 0.0 copy-done.9
  482.7 2.6 scatter_custom_fusion
  485.3 12.2 %gather_fusion.1 = f32[512,4096]{1,0:T(8,128)} fusion(f32[512,4096]{1,0:T(8,128)} %fusion.19, s32[1024]{0:T(1024)S(1)} %pad_clamp_fusion), kind=kCustom, calls=%fused_computation.1 | custom fusion | bytes 16779264 | tf_op jit(solution)/shard_map/gather | solution.py:62
  497.5 11.4 %multiply_convert_fusion = (bf16[512,4096]{1,0:T(8,128)(2,1)}, f32[512,4096]{1,0:T(8,128)}) fusion(f32[512,4096]{1,0:T(8,128)} %gather_fusion.1, f32[512,4096]{1,0:T(8,128)} %get-tuple-element.26, f32[512]{0:T(512)S(1)} %get-tuple-element.16, f32[512]{0:T(512)S(1)} %get-tuple-element.13, f32[4096]{0:T(1024)S(1)} %get-tuple-element.7, ...), kind=kLoop, calls=%fused_computation.30 | loop fusion | flops 25165824 | bytes 29417472 | tf_op jit(solution)/shard_map/convert_element_type | solution.py:67
  509.0 12.2 %gather_fusion = f32[512,4096]{1,0:T(8,128)} fusion(f32[512,4096]{1,0:T(8,128)} %get-tuple-element.24, s32[1024]{0:T(1024)S(1)} %pad_clamp_fusion.1), kind=kCustom, calls=%fused_computation | custom fusion | bytes 16779264 | tf_op jit(solution)/shard_map/gather | solution.py:61
  521.2 0.0 copy-start.1
  521.2 7.3 multiply_convert_fusion.1
  528.5 0.0 copy-start.6
  528.5 2.0 copy-done.6
  530.5 0.0 copy-done.1
  530.5 0.0 copy-start.4
  530.5 3.4 fusion.58
  533.9 0.0 copy-done.4
  533.9 3.4 fusion.56
  537.3 0.0 copy-start.8
  537.3 0.0 all-reduce.12.cloned.1.call-update
  537.4 0.0 all-reduce.10.cloned.1.call-start
  537.4 0.0 copy-start.5
  537.4 4.9 fusion.47
  542.3 0.0 copy-done.8
  542.3 0.0 copy-done.5
  542.3 6.1 convolution_add_fusion
  548.4 0.0 all-reduce.10.cloned.1.call-update
  548.4 48.4 %all-reduce.12.cloned.1.call-done = (f32[512,512]{1,0:T(8,128)}, f32[512,512]{1,0:T(8,128)}) async-done(((f32[512,512]{1,0:T(8,128)}, f32[512,512]{1,0:T(8,128)}), (f32[512,512]{1,0:T(8,128)}, f32[512,512]{1,0:T(8,128)})) %all-reduce.12.cloned.1.call-update) | async-done | bytes 2097168 | tf_op jit(solution)/shard_map/psum | solution.py:72
  596.8 1.5 fusion.43
  598.3 1.5 fusion.39
  599.8 2.4 fusion.45
  602.3 2.4 fusion.41
  604.7 116.6 %all-reduce.10.cloned.1.call-done = f32[4096,512]{1,0:T(8,128)} async-done(((f32[4096,512]{1,0:T(8,128)}), f32[4096,512]{1,0:T(8,128)}) %all-reduce.10.cloned.1.call-update) | async-done | bytes 8388624 | tf_op jit(solution)/shard_map/psum | solution.py:80
  721.3 0.0 copy-start.2
  721.3 0.0 copy-start.3
  721.3 6.1 fusion.15
  727.4 0.0 copy-done.2
  727.4 2.1 copy-done.3
  729.6 4.6 fusion.17
  (8 shorter events, 0.0 us)
Async XLA Ops:
  7.2 589.7 %all-reduce.12.cloned.1.call-start = ((), (), s32[]{:S(2)}) async-start(), calls=%async_computation.1 | async-start | bytes 4194304 | tf_op jit(solution)/shard_map/psum | solution.py:72
  12.8 8.5 %copy-start = (bf16[4096,512]{1,0:T(8,128)(2,1)S(1)}, bf16[4096,512]{1,0:T(8,128)(2,1)}, u32[]{:S(2)}) copy-start(bf16[4096,512]{1,0:T(8,128)(2,1)} %param.6) | copy-start | bytes 12582916
  12.8 8.5 %copy-start.7 = (bf16[512,512]{1,0:T(8,128)(2,1)S(1)}, bf16[512,512]{1,0:T(8,128)(2,1)}, u32[]{:S(2)}) copy-start(bf16[512,512]{1,0:T(8,128)(2,1)} %param.4) | copy-start | bytes 1572868
  475.3 7.4 copy-start.9
  521.2 9.3 %copy-start.1 = (bf16[4096,512]{1,0:T(8,128)(2,1)S(1)}, bf16[4096,512]{1,0:T(8,128)(2,1)}, u32[]{:S(2)}) copy-start(bf16[4096,512]{1,0:T(8,128)(2,1)} %param.6) | copy-start | bytes 12582916
  528.5 2.0 copy-start.6
  530.5 3.4 copy-start.4
  537.3 4.9 copy-start.8
  537.4 183.9 %all-reduce.10.cloned.1.call-start = ((), (), s32[]{:S(2)}) async-start(), calls=%async_computation | async-start | bytes 16777216 | tf_op jit(solution)/shard_map/psum | solution.py:80
  537.4 4.9 copy-start.5
  721.3 6.2 copy-start.2
  721.3 8.3 %copy-start.3 = (f32[4096,512]{1,0:T(8,128)S(1)}, f32[4096,512]{1,0:T(8,128)}, u32[]{:S(2)}) copy-start(f32[4096,512]{1,0:T(8,128)} %all-reduce.10.cloned.1.call-done) | copy-start | bytes 25165828
Sparse Core Ops, SparseCore 0:
  537.5 59.2 all-reduce.11
  601.1 120.0 all-reduce.9
where the time goes:
time: 749 us; the launch traced here: 741 us
  blocking collectives  401 us (54%)
  waiting for transfers between devices  165 us (22%)
  other arithmetic  98.8 us (13%)
  local copies, waits for them, and re-layouts  31.2 us (4%)
  matrix products  31.2 us (4%)
  between operations  14.5 us (2%)
    psum x3, blocking collectives, balance_single(): lax.psum(jnp.sum(codes, 0, keepdims=True), ('batch', 'replica'))  377 us
    psum x1, waiting for transfers between devices, per_device(): dunit_proto = lax.psum(local_grad, ('batch', 'replica'))  117 us
    psum x1, waiting for transfers between devices, per_device(): dunit_one, dunit_two = lax.psum((part_one, part_two), 'proto')  48.4 us
    psum x3, blocking collectives, balance_single(): codes = codes / lax.psum(jnp.sum(codes, 1, keepdims=True), 'proto')  23.6 us
    reduce_sum x4, other arithmetic, balance_single(): codes = codes / lax.psum(jnp.sum(codes, 1, keepdims=True), 'proto')  21.2 us
    reduce_sum x4, other arithmetic, balance_single(): jnp.sum(codes, 0, keepdims=True)  19.2 us
  transfers between devices with their start and end apart: 2, of which 2 were waited for; matrix products, arithmetic and copies ran while one was open for 3% of the time, Pallas kernels for 0%

commit v1 on v0

v1 whole, which is shorter than its diff:
```python
import functools

import jax
import jax.numpy as jnp
from jax import lax
from jax.experimental import pallas as pl
from jax.experimental.pallas import tpu as pltpu
from jax.sharding import PartitionSpec as P

ITERS = 3
EPS = 1e-06
F32 = jnp.float32
BF16 = jnp.bfloat16
MESH = pl.DeviceIdType.MESH
NN = (((1,), (0,)), ((), ()))
NT = (((1,), (1,)), ((), ()))
TN = (((0,), (0,)), ((), ()))
LOG2E = 1.4426950408889634


def dot(a, b, dims):
    return lax.dot_general(a, b, dims, preferred_element_type=F32)


def here():
    batch = lax.axis_index("batch")
    return lax.div(batch, 2), lax.rem(batch, 2), lax.axis_index("replica"), lax.axis_index("proto")


def greet(peers):
    barrier = pltpu.get_barrier_semaphore()
    for peer in peers:
        pl.semaphore_signal(barrier, inc=1, device_id=peer, device_id_type=MESH)
    pl.semaphore_wait(barrier, len(peers))


def send(src, dst, send_sem, recv_sem, peer):
    copy = pltpu.make_async_remote_copy(
        src_ref=src, dst_ref=dst, send_sem=send_sem, recv_sem=recv_sem,
        device_id=peer, device_id_type=MESH,
    )
    copy.start()
    return copy


def balance_kernel(
    nx, ny, nz,
    one_ref, two_ref, proto_ref, pair_ref,
    dproto_ref, dunit_ref,
    expo, dscore, low_seg, low_seg_t, low_two, low_proto, onehot, row_scale, prob_scale,
    cols, cols_in, cols_y, weight, rows, rows_in, tile_u,
    send_sem, recv_sem,
):
    y, core, x, z = here()
    line = 2 * nx
    spot = core * nx + x

    def line_peer(step):
        other = lax.rem(spot + step, line)
        return other, (y * 2 + lax.div(other, nx), lax.rem(other, nx), z)

    def y_peer(step):
        return (lax.rem(y + step, ny) * 2 + core, x, z)

    def z_peer(step):
        return (y * 2 + core, x, lax.rem(z + step, nz))

    greet(
        [line_peer(s)[1] for s in range(1, line)]
        + [y_peer(s) for s in range(1, ny)]
        + [z_peer(s) for s in range(1, nz)]
    )

    segs = one_ref.shape[0]
    protos, width = low_proto.shape
    both = 2 * segs

    def unit(block):
        xf = block.astype(F32)
        inv = lax.rsqrt(jnp.sum(xf * xf, -1, keepdims=True) + EPS)
        return (xf * inv).astype(BF16)

    def norm_views(i, carry):
        at = pl.ds(pl.multiple_of(i * 128, 128), 128)
        low_seg[at, :] = unit(one_ref[at, :])
        low_two[at, :] = unit(two_ref[at, :])
        return carry

    lax.fori_loop(0, segs // 128, norm_views, 0)
    pair = jnp.broadcast_to(pair_ref[...], (segs, segs))
    number = lax.broadcasted_iota(jnp.int32, (segs, segs), 0)
    onehot[...] = jnp.where(pair == number, 1.0, 0.0).astype(BF16)
    low_seg[segs:both, :] = dot(onehot[...], low_two[...], TN).astype(BF16)
    for i in range(both // 128):
        block = low_seg[i * 128:(i + 1) * 128, :].astype(F32)
        low_seg_t[:, i * 128:(i + 1) * 128] = jnp.transpose(block).astype(BF16)

    def norm_protos(i, carry):
        at = pl.ds(pl.multiple_of(i * 128, 128), 128)
        low_proto[at, :] = unit(proto_ref[at, :])
        return carry

    lax.fori_loop(0, protos // 128, norm_protos, 0)

    wide = protos // 4

    def scores(j, carry):
        for q in range(wide // 256):
            at = pl.ds(pl.multiple_of(j * wide + q * 256, 256), 256)
            s = dot(low_seg[...], low_proto[at, :], NT)
            e = jnp.exp2(s * (10.0 * LOG2E))
            expo[:, at] = e
            k = e * e
            for view in range(2):
                total = jnp.sum(k[view * segs:(view + 1) * segs], axis=0, keepdims=True)
                for h in range(2):
                    cols[0, view * 4 + j, q * 2 + h:q * 2 + h + 1, :] = total[:, h * 128:(h + 1) * 128]
        return carry

    lax.fori_loop(0, 4, scores, 0)

    def col_sums(it):
        def block(k, carry):
            first = pl.multiple_of(lax.div(k, 4) * segs, segs)
            left = lax.rem(k, 4) * wide

            def some(r, acc):
                acc = list(acc)
                for t in range(4):
                    at = pl.ds(pl.multiple_of(first + r * 32 + t * 8, 8), 8)
                    u = row_scale[at, :]
                    for l in range(wide // 128):
                        e = expo[at, pl.ds(pl.multiple_of(left + l * 128, 128), 128)]
                        acc[l] = acc[l] + (e * e) * u
                return tuple(acc)

            zero = jnp.zeros((8, 128), F32)
            acc = lax.fori_loop(0, segs // 32, some, (zero,) * (wide // 128))
            for l in range(wide // 128):
                cols[it, k, l:l + 1, :] = jnp.sum(acc[l], axis=0, keepdims=True)
            return carry

        lax.fori_loop(0, 8, block, 0)

    def all_cols(it):
        copies = []
        for s in range(1, line):
            other, peer = line_peer(s)
            copies.append(send(cols.at[it, other], cols_in.at[it, spot],
                               send_sem.at[it, s - 1], recv_sem.at[it, s - 1], peer))
        cols_in[it, spot] = cols[it, spot]
        for copy in copies:
            copy.wait()
        total = cols_in[it, 0]
        for k in range(1, line):
            total = total + cols_in[it, k]
        cols_y[it, y] = total
        copies = []
        for s in range(1, ny):
            copies.append(send(cols_y.at[it, y], cols_y.at[it, y],
                               send_sem.at[it, 7 + s - 1], recv_sem.at[it, 7 + s - 1], y_peer(s)))
        for copy in copies:
            copy.wait()
        total = cols_y[it, 0]
        for k in range(1, ny):
            total = total + cols_y[it, k]
        weight[it, spot] = 1.0 / total
        copies = []
        for s in range(1, line):
            copies.append(send(weight.at[it, spot], weight.at[it, spot],
                               send_sem.at[it, 10 + s - 1], recv_sem.at[it, 10 + s - 1], line_peer(s)[1]))
        for copy in copies:
            copy.wait()

    def row_sums(it, with_total):
        def block(b, carry):
            at = pl.ds(pl.multiple_of(b * 128, 128), 128)
            view = lax.div(b, 4)
            acc = jnp.zeros((128, 128), F32)
            tot = jnp.zeros((128, 128), F32)
            for l in range(protos // 128):
                e = expo[at, l * 128:(l + 1) * 128]
                v = weight[it, view * 4 + l // 8, l % 8:l % 8 + 1, :]
                acc = acc + (e * e) * v
                if with_total:
                    tot = tot + e
            rows[it, pl.ds(b, 1), :] = jnp.sum(jnp.transpose(acc), axis=0, keepdims=True)
            if with_total:
                rows[it, pl.ds(8 + b, 1), :] = jnp.sum(jnp.transpose(tot), axis=0, keepdims=True)
            return carry

        lax.fori_loop(0, 8, block, 0)

    def spread(out, row):
        def block(b, carry):
            at = pl.ds(pl.multiple_of(b * 128, 128), 128)
            out[at, :] = jnp.transpose(jnp.broadcast_to(tile_u[pl.ds(row + b, 1), :], (128, 128)))
            return carry

        lax.fori_loop(0, 8, block, 0)

    def all_rows(it, with_total, scale):
        size = 16 if with_total else 8
        rows_in[it, z] = rows[it]
        copies = []
        for s in range(1, nz):
            copies.append(send(rows.at[it, 0:size], rows_in.at[it, z, 0:size],
                               send_sem.at[it, 17 + s - 1], recv_sem.at[it, 17 + s - 1], z_peer(s)))
        for copy in copies:
            copy.wait()
        total = rows_in[it, 0, 0:size]
        for k in range(1, nz):
            total = total + rows_in[it, k, 0:size]
        tile_u[0:8, :] = scale / total[0:8]
        spread(row_scale, 0)
        if with_total:
            tile_u[8:16, :] = 5.0 / total[8:16]
            spread(prob_scale, 8)

    for it in range(ITERS):
        if it:
            col_sums(it)
        all_cols(it)
        row_sums(it, it == 0)
        all_rows(it, it == 0, 5.0 if it == ITERS - 1 else 1.0)

    last = ITERS - 1

    def grads(j, carry):
        for h in range(2):
            at = pl.ds(pl.multiple_of(j * 256 + h * 128, 128), 128)
            tile = lax.div(j, 4)
            row = lax.rem(j, 4) * 2 + h
            v_one = weight[last, tile, pl.ds(row, 1), :]
            v_two = weight[last, 4 + tile, pl.ds(row, 1), :]
            for b in range(segs // 64):
                first = slice(b * 64, (b + 1) * 64)
                second = slice(segs + b * 64, segs + (b + 1) * 64)
                e_one = expo[first, at]
                e_two = expo[second, at]
                t_one = (e_two * e_two) * row_scale[second, :] * v_two
                t_two = (e_one * e_one) * row_scale[first, :] * v_one
                dscore[first, at] = (e_one * prob_scale[first, :] - t_one).astype(BF16)
                dscore[second, at] = (e_two * prob_scale[second, :] - t_two).astype(BF16)
        at = pl.ds(pl.multiple_of(j * 256, 256), 256)
        part = dot(low_seg_t[...], dscore[:, at], NN)
        dproto_ref[2 * j] = part[:, 0:128]
        dproto_ref[2 * j + 1] = part[:, 128:256]
        return carry

    lax.fori_loop(0, protos // 256, grads, 0)

    def views(i, carry):
        at = pl.ds(pl.multiple_of(i * 256, 256), 256)
        dunit_ref[at, :] = dot(dscore[at, :], low_proto[...], NN)
        return carry

    lax.fori_loop(0, both // 256, views, 0)
    d = dunit_ref[segs:both, :]
    high = d.astype(BF16)
    rest = d - high.astype(F32)
    mid = rest.astype(BF16)
    low = (rest - mid.astype(F32)).astype(BF16)
    tail = dot(onehot[...], mid, NN) + dot(onehot[...], low, NN)
    dunit_ref[segs:both, :] = dot(onehot[...], high, NN) + tail


def balance(mesh, one, two, protos, pair):
    nx, ny, nz = mesh.shape["replica"], mesh.shape["batch"] // 2, mesh.shape["proto"]
    segs, width = one.shape
    count = protos.shape[0]
    both = 2 * segs
    vmem = pl.BlockSpec(memory_space=pltpu.VMEM)
    return pl.pallas_call(
        functools.partial(balance_kernel, nx, ny, nz),
        out_shape=(
            jax.ShapeDtypeStruct((count // 128, width, 128), F32),
            jax.ShapeDtypeStruct((both, width), F32),
        ),
        in_specs=[vmem] * 4,
        out_specs=(vmem, vmem),
        scratch_shapes=[
            pltpu.VMEM((both, count), F32),
            pltpu.VMEM((both, count), BF16),
            pltpu.VMEM((both, width), BF16),
            pltpu.VMEM((width, both), BF16),
            pltpu.VMEM((segs, width), BF16),
            pltpu.VMEM((count, width), BF16),
            pltpu.VMEM((segs, segs), BF16),
            pltpu.VMEM((both, 128), F32),
            pltpu.VMEM((both, 128), F32),
            pltpu.VMEM((ITERS, 8, 8, 128), F32),
            pltpu.VMEM((ITERS, 8, 8, 128), F32),
            pltpu.VMEM((ITERS, ny, 8, 128), F32),
            pltpu.VMEM((ITERS, 8, 8, 128), F32),
            pltpu.VMEM((ITERS, 16, 128), F32),
            pltpu.VMEM((ITERS, nz, 16, 128), F32),
            pltpu.VMEM((16, 128), F32),
            pltpu.SemaphoreType.DMA((ITERS, 20)),
            pltpu.SemaphoreType.DMA((ITERS, 20)),
        ],
        compiler_params=pltpu.CompilerParams(
            collective_id=0, has_side_effects=True, vmem_limit_bytes=60 << 20
        ),
        name="balance",
    )(one, two, protos, pair)


def unit_rows(x):
    xf = x.astype(F32)
    inv = lax.rsqrt(jnp.sum(xf * xf, -1, keepdims=True) + EPS)
    return xf * inv, inv


def unit_back(grad, x):
    unit, inv = unit_rows(x)
    return inv * (grad - unit * jnp.sum(unit * grad, -1, keepdims=True))


def per_device(mesh, view_one, view_two, prototypes, pairing):
    dproto, dunit = balance(mesh, view_one, view_two, prototypes, pairing)
    dunit = lax.psum(dunit, "proto")
    dproto = lax.psum(dproto, ("batch", "replica"))
    dproto = jnp.swapaxes(dproto, 1, 2).reshape(prototypes.shape)
    segs = view_one.shape[0]
    return (
        unit_back(dunit[:segs], view_one),
        unit_back(dunit[segs:], view_two),
        unit_back(dproto, prototypes),
    )


def solution(mesh):
    rows = P(("batch", "replica"), None)
    protos = P("proto", None)
    return jax.shard_map(
        functools.partial(per_device, mesh),
        mesh=mesh,
        in_specs=(rows, rows, protos, rows),
        out_specs=(rows, rows, protos),
        check_vma=False,
    )
```

time: 749 us -> 314 us (0.42)
  blocking collectives: 401 us -> 0 us
  Pallas kernels: 0 us -> 105 us
  other arithmetic: 98.8 us -> 19.6 us
  matrix products: 31.2 us -> 0 us
  local copies, waits for them, and re-layouts: 31.2 us -> 12.3 us
    psum x6 -> x0, blocking collectives: 401 us -> none  [the longest x3 377 us: balance_single(): lax.psum(jnp.sum(codes, 0, keepdims=True), ('batch', 'replica'))]
    pallas_call x0 -> x1, Pallas kernels: none -> 105 us  [balance(): pl.pallas_call(functools.partial(balance_kernel, nx, ny, nz), out_shape=(...]
    reduce_sum x12 -> x3, other arithmetic: 54 us -> 3.47 us  [unit_rows(): inv = lax.rsqrt(jnp.sum(xf * xf, -1, keepdims=True) + EPS)]
    dot_general x6 -> x0, matrix products: 31.2 us -> none  [the longest x1 8.45 us: per_device(): lax.dot_general(low_two, low_proto, dims, preferred_element_type=jnp.floa...]
    gather x2 -> x0, local copies, waits for them, and re-layouts: 24.4 us -> none  [the longest x1 12.2 us: per_device(): target_two = codes_one[inverse]]
    convert_element_type x2 -> x0, other arithmetic: 18.7 us -> none  [the longest x1 11.4 us: per_device(): (gradient_scale_factor * (exponent_second_view / total_two - target_two))...]
    transpose x0 -> x1, local copies, waits for them, and re-layouts: none -> 9.13 us  [per_device(): dproto = jnp.swapaxes(dproto, 1, 2).reshape(prototypes.shape)]
  transfers between devices with their start and end apart: 2 -> 2, of which waited for: 2 -> 2; matrix products, arithmetic and copies ran while one was open for 3% -> 6% of each run, Pallas kernels for 0% -> 0%
where the time goes in v1:
time: 314 us; the launch traced here: 313 us
  waiting for transfers between devices  163 us (52%)
  Pallas kernels  105 us (33%)
  other arithmetic  19.6 us (6%)
  between operations  14.1 us (4%)
  local copies, waits for them, and re-layouts  12.3 us (4%)
    psum x1, waiting for transfers between devices, per_device(): dproto = lax.psum(dproto, ('batch', 'replica'))  119 us
    pallas_call x1, Pallas kernels, balance(): pl.pallas_call(functools.partial(balance_kernel, nx, ny, nz), out_shape=(...  105 us
    psum x1, waiting for transfers between devices, per_device(): dunit = lax.psum(dunit, 'proto')  43.5 us
    transpose x1, local copies, waits for them, and re-layouts, per_device(): dproto = jnp.swapaxes(dproto, 1, 2).reshape(prototypes.shape)  9.13 us
    reduce_sum x2, other arithmetic, unit_back(): return inv * (grad - unit * jnp.sum(unit * grad, -1, keepdims=True))  8.16 us
    mul x2, other arithmetic, unit_back(): return inv * (grad - unit * jnp.sum(unit * grad, -1, keepdims=True))  7.93 us
  transfers between devices with their start and end apart: 2, of which 2 were waited for; matrix products, arithmetic and copies ran while one was open for 6% of the time, Pallas kernels for 0%

profile of v1, /device:TPU:1, one launch (start us, length us, event | category | flops | bytes accessed | tf_op | source)
XLA Modules:
  0.0 313.5 jit_solution(273378157303269580)
XLA Ops:
  7.2 0.0 all-reduce.3.cloned.1.call-start
  7.2 104.7 %balance.1 = (f32[32,512,128]{2,1,0:T(8,128)}, f32[1024,512]{1,0:T(8,128)}) custom-call(bf16[512,512]{1,0:T(8,128)(2,1)} %one_ref.1, bf16[512,512]{1,0:T(8,128)(2,1)} %two_ref.1, bf16[4096,512]{1,0:T(8,128)(2,1)} %proto_ref.1, s32[1,512]{1,0:T(1,128)} %pair_ref.1), custom_call_target="tpu_custom_call" | custom-call | tf_op jit(solution)/shard_map/balance/pallas_call | solution.py:274
  111.9 0.0 all-reduce.3.cloned.1.call-update
  112.0 0.0 all-reduce.5.cloned.1.call-start
  112.0 9.1 %copy.7 = f32[32,128,512]{2,1,0:T(8,128)} copy(f32[32,128,512]{1,2,0:T(8,128)} %bitcast.3) | data formatting | bytes 16777216 | tf_op jit(solution)/shard_map/transpose | solution.py:324
  121.1 0.0 copy-start.3
  121.1 0.0 copy-start.2
  121.1 0.0 all-reduce.5.cloned.1.call-update
  121.2 1.0 copy-done.3
  122.2 0.2 fusion.16
  122.4 0.0 copy-done.2
  122.4 0.2 fusion.17
  122.6 3.1 fusion.5
  125.7 43.5 %all-reduce.3.cloned.1.call-done = f32[1024,512]{1,0:T(8,128)} async-done(((f32[1024,512]{1,0:T(8,128)}), f32[1024,512]{1,0:T(8,128)}) %all-reduce.3.cloned.1.call-update) | async-done | bytes 2097168 | tf_op jit(solution)/shard_map/psum | solution.py:322
  169.2 2.0 fusion.10
  171.2 3.3 %fusion.12 = (f32[512,512]{1,0:T(8,128)}, f32[512,512]{1,0:T(8,128)}) fusion(bf16[512,512]{1,0:T(8,128)(2,1)S(1)} %copy-done.2, f32[1024,512]{1,0:T(8,128)} %all-reduce.3.cloned.1.call-done, f32[512]{0:T(512)S(1)} %get-tuple-element.7, f32[512]{0:T(512)S(1)} %get-tuple-element.11, f32[512]{0:T(512)S(1)} %get-tuple-element.8, ...), kind=kLoop, calls=%fused_computation.18 | loop fusion | flops 2621440 | bytes 5251072 | tf_op jit(solution)/shard_map/mul | solution.py:317
  174.5 119.2 %all-reduce.5.cloned.1.call-done = f32[4096,512]{1,0:T(8,128)} async-done(((f32[4096,512]{1,0:T(8,128)}), f32[4096,512]{1,0:T(8,128)}) %all-reduce.5.cloned.1.call-update) | async-done | bytes 8388624 | tf_op jit(solution)/shard_map/psum | solution.py:323
  293.7 0.0 copy-start
  293.7 0.0 copy-start.1
  293.7 6.2 %fusion.2 = f32[4096]{0:T(1024)S(1)} fusion(f32[4096,512]{1,0:T(8,128)} %all-reduce.5.cloned.1.call-done, bf16[4096,512]{1,0:T(8,128)(2,1)} %proto_ref.1, f32[4096]{0:T(1024)S(1)} %add_rsqrt_fusion), kind=kLoop, calls=%fused_computation.4 | loop fusion | flops 8384512 | bytes 12615680 | tf_op jit(solution)/shard_map/reduce_sum | solution.py:317
  299.8 0.0 copy-done
  299.9 2.1 copy-done.1
  302.0 4.7 %fusion.4 = f32[4096,512]{1,0:T(8,128)} fusion(f32[4096,512]{1,0:T(8,128)S(1)} %copy-done.1, bf16[4096,512]{1,0:T(8,128)(2,1)S(1)} %copy-done, f32[4096]{0:T(1024)S(1)} %fusion.2, f32[4096]{0:T(1024)S(1)} %add_rsqrt_fusion), kind=kLoop, calls=%fused_computation.6 | loop fusion | flops 10485760 | bytes 21004288 | tf_op jit(solution)/shard_map/mul | solution.py:317
  (2 shorter events, 0.0 us)
Async XLA Ops:
  7.2 162.0 %all-reduce.3.cloned.1.call-start = ((), (), s32[]{:S(2)}) async-start(), calls=%async_computation | async-start | bytes 4194304 | tf_op jit(solution)/shard_map/psum | solution.py:322
  112.0 181.7 %all-reduce.5.cloned.1.call-start = ((), (), s32[]{:S(2)}) async-start(), calls=%async_computation.1 | async-start | bytes 16777216 | tf_op jit(solution)/shard_map/psum | solution.py:323
  121.1 1.0 copy-start.3
  121.1 1.2 copy-start.2
  293.7 6.2 %copy-start = (bf16[4096,512]{1,0:T(8,128)(2,1)S(1)}, bf16[4096,512]{1,0:T(8,128)(2,1)}, u32[]{:S(2)}) copy-start(bf16[4096,512]{1,0:T(8,128)(2,1)} %proto_ref.1) | copy-start | bytes 12582916
  293.7 8.3 %copy-start.1 = (f32[4096,512]{1,0:T(8,128)S(1)}, f32[4096,512]{1,0:T(8,128)}, u32[]{:S(2)}) copy-start(f32[4096,512]{1,0:T(8,128)} %all-reduce.5.cloned.1.call-done) | copy-start | bytes 25165828
Sparse Core Ops, SparseCore 0:
  112.1 57.0 all-reduce.2
  173.5 120.1 all-reduce.4

commit v2 on v1

v2 whole, which is shorter than its diff:
```python
import functools

import jax
import jax.numpy as jnp
from jax import lax
from jax.experimental import pallas as pl
from jax.experimental.pallas import tpu as pltpu
from jax.sharding import PartitionSpec as P

ITERS = 3
EPS = 1e-06
F32 = jnp.float32
BF16 = jnp.bfloat16
MESH = pl.DeviceIdType.MESH
NN = (((1,), (0,)), ((), ()))
NT = (((1,), (1,)), ((), ()))
TN = (((0,), (0,)), ((), ()))
LOG2E = 1.4426950408889634


def dot(a, b, dims):
    return lax.dot_general(a, b, dims, preferred_element_type=F32)


def here():
    batch = lax.axis_index("batch")
    return lax.div(batch, 2), lax.rem(batch, 2), lax.axis_index("replica"), lax.axis_index("proto")


class Links:
    def __init__(self, send_sem, recv_sem):
        self.send_sem, self.recv_sem, self.used, self.sent = send_sem, recv_sem, 0, []

    def send(self, src, dst, peer):
        copy = pltpu.make_async_remote_copy(
            src_ref=src, dst_ref=dst,
            send_sem=self.send_sem.at[self.used], recv_sem=self.recv_sem.at[self.used],
            device_id=peer, device_id_type=MESH,
        )
        copy.start()
        self.used += 1
        self.sent.append(copy)
        return copy

    def drain(self):
        for copy in self.sent:
            copy.wait_send()
        self.sent = []


def back(d, raw):
    xf = raw.astype(F32)
    inv = lax.rsqrt(jnp.sum(xf * xf, -1, keepdims=True) + EPS)
    u = xf * inv
    return inv * (d - u * jnp.sum(u * d, -1, keepdims=True))


def balance_kernel(
    nx, ny, nz,
    one_hbm, two_hbm, proto_hbm, pair_ref,
    gview_hbm, gproto_hbm,
    raw, expo, dscore, low_seg, low_seg_t, low_two, low_proto, onehot, row_scale, prob_scale,
    cols, cols_in, cols_y, weight, rows, rows_in, tile_u,
    dproto, from_core, dunit, own_proto, gproto, gview,
    a_relay, a_plain, a_joint, b_relay, b_plain, b_joint, z_relay, z_plain, z_joint,
    send_sem, recv_sem, local_sem,
):
    y, core, x, z = here()
    line = 2 * nx
    spot = core * nx + x
    links = Links(send_sem, recv_sem)
    at_a = core * y + (1 - core) * x
    at_b = core * x + (1 - core) * y
    mine = core * 16 + at_a * 4 + at_b

    def line_peer(step):
        other = lax.rem(spot + step, line)
        return other, (y * 2 + lax.div(other, nx), lax.rem(other, nx), z)

    def y_peer(step):
        return (lax.rem(y + step, ny) * 2 + core, x, z)

    def z_peer(step):
        return (y * 2 + core, x, lax.rem(z + step, nz))

    def a_peer(step):
        return (lax.rem(y + core * step, ny) * 2 + core, lax.rem(x + (1 - core) * step, nx), z)

    def b_peer(step):
        return (lax.rem(y + (1 - core) * step, ny) * 2 + core, lax.rem(x + core * step, nx), z)

    sibling = (y * 2 + 1 - core, x, z)

    segs = one_hbm.shape[0]
    protos, width = low_proto.shape
    both = 2 * segs
    fetch = [
        pltpu.make_async_copy(one_hbm, raw.at[0:segs], local_sem.at[0]),
        pltpu.make_async_copy(two_hbm, raw.at[segs:both], local_sem.at[1]),
        pltpu.make_async_copy(proto_hbm, low_proto, local_sem.at[2]),
        pltpu.make_async_copy(proto_hbm.at[pl.ds(mine * 128, 128)], own_proto, local_sem.at[3]),
    ]
    for copy in fetch:
        copy.start()
    peers = (
        [line_peer(s)[1] for s in range(1, line)]
        + [y_peer(s) for s in range(1, ny)]
        + [z_peer(s) for s in range(1, nz)]
    )
    barrier = pltpu.get_barrier_semaphore()
    for peer in peers:
        pl.semaphore_signal(barrier, inc=1, device_id=peer, device_id_type=MESH)

    def unit(block):
        xf = block.astype(F32)
        inv = lax.rsqrt(jnp.sum(xf * xf, -1, keepdims=True) + EPS)
        return (xf * inv).astype(BF16)

    def norm_views(i, carry):
        at = pl.ds(pl.multiple_of(i * 128, 128), 128)
        low_seg[at, :] = unit(raw[at, :])
        low_two[at, :] = unit(raw[pl.ds(pl.multiple_of(segs + i * 128, 128), 128), :])
        return carry

    fetch[0].wait()
    fetch[1].wait()
    lax.fori_loop(0, segs // 128, norm_views, 0)
    pair = jnp.broadcast_to(pair_ref[...], (segs, segs))
    number = lax.broadcasted_iota(jnp.int32, (segs, segs), 0)
    onehot[...] = jnp.where(pair == number, 1.0, 0.0).astype(BF16)
    low_seg[segs:both, :] = dot(onehot[...], low_two[...], TN).astype(BF16)
    for i in range(both // 128):
        block = low_seg[i * 128:(i + 1) * 128, :].astype(F32)
        low_seg_t[:, i * 128:(i + 1) * 128] = jnp.transpose(block).astype(BF16)

    def norm_protos(i, carry):
        at = pl.ds(pl.multiple_of(i * 128, 128), 128)
        low_proto[at, :] = unit(low_proto[at, :])
        return carry

    fetch[2].wait()
    lax.fori_loop(0, protos // 128, norm_protos, 0)

    wide = protos // 4

    def scores(j, carry):
        for q in range(wide // 256):
            at = pl.ds(pl.multiple_of(j * wide + q * 256, 256), 256)
            s = dot(low_seg[...], low_proto[at, :], NT)
            e = jnp.exp2(s * (10.0 * LOG2E))
            expo[:, at] = e
            k = e * e
            for view in range(2):
                total = jnp.sum(k[view * segs:(view + 1) * segs], axis=0, keepdims=True)
                for h in range(2):
                    cols[0, view * 4 + j, q * 2 + h:q * 2 + h + 1, :] = total[:, h * 128:(h + 1) * 128]
        return carry

    lax.fori_loop(0, 4, scores, 0)

    def col_sums(it):
        def block(k, carry):
            first = pl.multiple_of(lax.div(k, 4) * segs, segs)
            left = lax.rem(k, 4) * wide

            def some(r, acc):
                acc = list(acc)
                for t in range(4):
                    at = pl.ds(pl.multiple_of(first + r * 32 + t * 8, 8), 8)
                    u = row_scale[at, :]
                    for l in range(wide // 128):
                        e = expo[at, pl.ds(pl.multiple_of(left + l * 128, 128), 128)]
                        acc[l] = acc[l] + (e * e) * u
                return tuple(acc)

            zero = jnp.zeros((8, 128), F32)
            acc = lax.fori_loop(0, segs // 32, some, (zero,) * (wide // 128))
            for l in range(wide // 128):
                cols[it, k, l:l + 1, :] = jnp.sum(acc[l], axis=0, keepdims=True)
            return carry

        lax.fori_loop(0, 8, block, 0)

    def all_cols(it):
        copies = []
        for s in range(1, line):
            other, peer = line_peer(s)
            copies.append(links.send(cols.at[it, other], cols_in.at[it, spot], peer))
        cols_in[it, spot] = cols[it, spot]
        for copy in copies:
            copy.wait_recv()
        total = cols_in[it, 0]
        for k in range(1, line):
            total = total + cols_in[it, k]
        cols_y[it, y] = total
        copies = []
        for s in range(1, ny):
            copies.append(links.send(cols_y.at[it, y], cols_y.at[it, y], y_peer(s)))
        for copy in copies:
            copy.wait_recv()
        total = cols_y[it, 0]
        for k in range(1, ny):
            total = total + cols_y[it, k]
        weight[it, spot] = 1.0 / total
        copies = []
        for s in range(1, line):
            copies.append(links.send(weight.at[it, spot], weight.at[it, spot], line_peer(s)[1]))
        for copy in copies:
            copy.wait_recv()

    def row_sums(it, with_total):
        def block(b, carry):
            at = pl.ds(pl.multiple_of(b * 128, 128), 128)
            view = lax.div(b, 4)
            acc = jnp.zeros((128, 128), F32)
            tot = jnp.zeros((128, 128), F32)
            for l in range(protos // 128):
                e = expo[at, l * 128:(l + 1) * 128]
                v = weight[it, view * 4 + l // 8, l % 8:l % 8 + 1, :]
                acc = acc + (e * e) * v
                if with_total:
                    tot = tot + e
            rows[it, pl.ds(b, 1), :] = jnp.sum(jnp.transpose(acc), axis=0, keepdims=True)
            if with_total:
                rows[it, pl.ds(8 + b, 1), :] = jnp.sum(jnp.transpose(tot), axis=0, keepdims=True)
            return carry

        lax.fori_loop(0, 8, block, 0)

    def spread(out, row):
        def block(b, carry):
            at = pl.ds(pl.multiple_of(b * 128, 128), 128)
            out[at, :] = jnp.transpose(jnp.broadcast_to(tile_u[pl.ds(row + b, 1), :], (128, 128)))
            return carry

        lax.fori_loop(0, 8, block, 0)

    def all_rows(it, with_total, scale):
        size = 16 if with_total else 8
        rows_in[it, z] = rows[it]
        copies = []
        for s in range(1, nz):
            copies.append(links.send(rows.at[it, 0:size], rows_in.at[it, z, 0:size], z_peer(s)))
        for copy in copies:
            copy.wait_recv()
        total = rows_in[it, 0, 0:size]
        for k in range(1, nz):
            total = total + rows_in[it, k, 0:size]
        tile_u[0:8, :] = scale / total[0:8]
        spread(row_scale, 0)
        if with_total:
            tile_u[8:16, :] = 5.0 / total[8:16]
            spread(prob_scale, 8)

    pl.semaphore_wait(barrier, len(peers))
    for it in range(ITERS):
        if it:
            col_sums(it)
        all_cols(it)
        row_sums(it, it == 0)
        all_rows(it, it == 0, 5.0 if it == ITERS - 1 else 1.0)

    last = ITERS - 1

    def group(half, a):
        first_chunk = half * 16 + a * 4

        def grads(j, carry):
            chunk = first_chunk + j * 2
            for h in range(2):
                at = pl.ds(pl.multiple_of((chunk + h) * 128, 128), 128)
                tile = lax.div(chunk, 8)
                row = lax.rem(chunk, 8) + h
                v_one = weight[last, tile, pl.ds(row, 1), :]
                v_two = weight[last, 4 + tile, pl.ds(row, 1), :]
                for b in range(segs // 64):
                    first = slice(b * 64, (b + 1) * 64)
                    second = slice(segs + b * 64, segs + (b + 1) * 64)
                    e_one = expo[first, at]
                    e_two = expo[second, at]
                    t_one = (e_two * e_two) * row_scale[second, :] * v_two
                    t_two = (e_one * e_one) * row_scale[first, :] * v_one
                    dscore[first, at] = (e_one * prob_scale[first, :] - t_one).astype(BF16)
                    dscore[second, at] = (e_two * prob_scale[second, :] - t_two).astype(BF16)
            at = pl.ds(pl.multiple_of(chunk * 128, 256), 256)
            part = dot(low_seg_t[...], dscore[:, at], NN)
            dproto[chunk] = part[:, 0:128]
            dproto[chunk + 1] = part[:, 128:256]
            return carry

        lax.fori_loop(0, 2, grads, 0)
        return first_chunk

    order = (2, 1, 3, 0)
    crossing = []
    for t in order:
        a = lax.rem(at_b + t, 4)
        first = group(1 - core, a)
        crossing.append(links.send(dproto.at[pl.ds(first, 4)], from_core.at[pl.ds(a * 4, 4)], sibling))
    relays, plains, joints = [None] * 2, [None] * 2, [None] * 2
    base = {}
    for t, arrival in zip(order, crossing):
        a = lax.rem(at_a + t, 4)
        first = group(core, a)
        base[t] = first
        arrival.wait_recv()
        for q in range(4):
            dproto[first + q] = dproto[first + q] + from_core[a * 4 + q]
        low, high = dproto.at[pl.ds(first, 2)], dproto.at[pl.ds(first + 2, 2)]
        if t == 2:
            relays = [links.send(low, a_relay.at[0], a_peer(1)), links.send(high, a_relay.at[1], a_peer(3))]
        if t == 1:
            plains[0] = links.send(high, a_plain.at[0], a_peer(1))
        if t == 3:
            plains[1] = links.send(low, a_plain.at[1], a_peer(3))

    def views(i):
        at = slice(i * 256, (i + 1) * 256)
        dunit[at, :] = dot(dscore[at, :], low_proto[...], NN)

    views(0)
    views(1)
    relays[0].wait_recv()
    for q in range(2):
        dproto[base[1] + q] = dproto[base[1] + q] + a_relay[0, q]
    joints[0] = links.send(dproto.at[pl.ds(base[1], 2)], a_joint.at[0], a_peer(1))
    relays[1].wait_recv()
    for q in range(2):
        dproto[base[3] + 2 + q] = dproto[base[3] + 2 + q] + a_relay[1, q]
    joints[1] = links.send(dproto.at[pl.ds(base[3] + 2, 2)], a_joint.at[1], a_peer(3))

    views(2)
    views(3)
    d = dunit[segs:both, :]
    top = d.astype(BF16)
    rest = d - top.astype(F32)
    middle = rest.astype(BF16)
    end = (rest - middle.astype(F32)).astype(BF16)
    rest = dot(onehot[...], middle, NN) + dot(onehot[...], end, NN)
    dunit[segs:both, :] = dot(onehot[...], top, NN) + rest

    def part(ref, k, size, lower):
        half = size // 2
        start = k * size + (0 if lower else half)
        return ref.at[pl.ds(pl.multiple_of(start, half), half)]

    seg_part = both // nz
    z_right, z_left, z_far = lax.rem(z + 1, 4), lax.rem(z + 3, 4), lax.rem(z + 2, 4)
    z_relays = [
        links.send(part(dunit, z_far, seg_part, True), z_relay.at[0], z_peer(1)),
        links.send(part(dunit, z_far, seg_part, False), z_relay.at[1], z_peer(3)),
    ]
    z_plains = [
        links.send(part(dunit, z_right, seg_part, False), z_plain.at[0], z_peer(1)),
        links.send(part(dunit, z_left, seg_part, True), z_plain.at[1], z_peer(3)),
    ]

    own = base[0]
    for copy in plains + joints:
        copy.wait_recv()
    for q in range(2):
        dproto[own + q] = dproto[own + q] + (a_joint[0, q] + a_plain[1, q])
        dproto[own + 2 + q] = dproto[own + 2 + q] + (a_plain[0, q] + a_joint[1, q])
    b_right, b_left, b_far = lax.rem(at_b + 1, 4), lax.rem(at_b + 3, 4), lax.rem(at_b + 2, 4)
    half = width // 2
    b_relays = [
        links.send(dproto.at[own + b_far, 0:half], b_relay.at[0], b_peer(1)),
        links.send(dproto.at[own + b_far, half:width], b_relay.at[1], b_peer(3)),
    ]
    b_plains = [
        links.send(dproto.at[own + b_right, half:width], b_plain.at[0], b_peer(1)),
        links.send(dproto.at[own + b_left, 0:half], b_plain.at[1], b_peer(3)),
    ]

    z_half = seg_part // 2
    z_joints = []
    for way, k, skip, peer in ((0, z_right, 0, z_peer(1)), (1, z_left, z_half, z_peer(3))):
        z_relays[way].wait_recv()
        at = pl.ds(pl.multiple_of(k * seg_part + skip, z_half), z_half)
        dunit[at, :] = dunit[at, :] + z_relay[way]
        z_joints.append(links.send(dunit.at[at], z_joint.at[way], peer))

    b_joints = []
    for way, k, skip, peer in ((0, b_right, 0, b_peer(1)), (1, b_left, half, b_peer(3))):
        b_relays[way].wait_recv()
        at = slice(skip, skip + half)
        dproto[own + k, at, :] = dproto[own + k, at, :] + b_relay[way]
        b_joints.append(links.send(dproto.at[own + k, at], b_joint.at[way], peer))
    for copy in b_plains + b_joints:
        copy.wait_recv()
    me = own + at_b
    dproto[me, 0:half, :] = dproto[me, 0:half, :] + (b_joint[0] + b_plain[1])
    dproto[me, half:width, :] = dproto[me, half:width, :] + (b_plain[0] + b_joint[1])
    fetch[3].wait()
    gproto[...] = back(jnp.transpose(dproto[me]), own_proto[...])

    def rows_of(chunk, part=None):
        if part is None:
            return gproto_hbm.at[pl.ds(pl.multiple_of(chunk * 128, 128), 128)]
        return gproto_hbm.at[pl.ds(pl.multiple_of(chunk * 128 + part * 64, 64), 64)]

    def chunk_of(a, b):
        return core * 16 + a * 4 + b

    across = []

    def to_sibling(place, src=None):
        across.append(links.send(place if src is None else src, place, sibling))

    b_whole = [links.send(gproto, rows_of(mine), b_peer(1)), links.send(gproto, rows_of(mine), b_peer(3))]
    a_whole = {0: [links.send(gproto, rows_of(mine), a_peer(1)), links.send(gproto, rows_of(mine), a_peer(3))]}
    to_sibling(rows_of(mine), gproto)
    keep = pltpu.make_async_copy(gproto, rows_of(mine), local_sem.at[4])
    keep.start()

    for copy in z_plains + z_joints:
        copy.wait_recv()
    at = pl.ds(pl.multiple_of(z * seg_part, z_half), z_half)
    dunit[at, :] = dunit[at, :] + (z_joint[0] + z_plain[1])
    at = pl.ds(pl.multiple_of(z * seg_part + z_half, z_half), z_half)
    dunit[at, :] = dunit[at, :] + (z_plain[0] + z_joint[1])
    at = pl.ds(pl.multiple_of(z * seg_part, seg_part), seg_part)
    gview[...] = back(dunit[at, :], raw[at, :])
    place = gview_hbm.at[at]
    z_whole = [links.send(gview, place, z_peer(1)), links.send(gview, place, z_peer(3))]
    keep_view = pltpu.make_async_copy(gview, place, local_sem.at[5])
    keep_view.start()

    b_halves, a_halves = [], {}
    a_right, a_left, a_far = lax.rem(at_a + 1, 4), lax.rem(at_a + 3, 4), lax.rem(at_a + 2, 4)

    def along_a(key, place):
        a_whole[key] = a_whole.get(key, []) + [links.send(place, place, a_peer(1)), links.send(place, place, a_peer(3))]
        to_sibling(place)

    b_whole[0].wait_recv()
    b_halves.append(links.send(rows_of(chunk_of(at_a, b_left), 0), rows_of(chunk_of(at_a, b_left), 0), b_peer(1)))
    along_a(3, rows_of(chunk_of(at_a, b_left)))
    b_whole[1].wait_recv()
    b_halves.append(links.send(rows_of(chunk_of(at_a, b_right), 1), rows_of(chunk_of(at_a, b_right), 1), b_peer(3)))
    along_a(1, rows_of(chunk_of(at_a, b_right)))

    def pass_on(key, b):
        left, right = chunk_of(a_left, b), chunk_of(a_right, b)
        a_whole[key][0].wait_recv()
        a_halves[key] = [links.send(rows_of(left, 0), rows_of(left, 0), a_peer(1))]
        to_sibling(rows_of(left))
        a_whole[key][1].wait_recv()
        a_halves[key].append(links.send(rows_of(right, 1), rows_of(right, 1), a_peer(3)))
        to_sibling(rows_of(right))

    pass_on(0, at_b)
    far = chunk_of(at_a, b_far)
    b_halves[0].wait_recv()
    b_halves[1].wait_recv()
    along_a(2, rows_of(far))

    z_left_place = gview_hbm.at[pl.ds(pl.multiple_of(z_left * seg_part, seg_part), z_half)]
    z_right_place = gview_hbm.at[pl.ds(pl.multiple_of(z_right * seg_part + z_half, z_half), z_half)]
    z_whole[0].wait_recv()
    z_halves = [links.send(z_left_place, z_left_place, z_peer(1))]
    z_whole[1].wait_recv()
    z_halves.append(links.send(z_right_place, z_right_place, z_peer(3)))

    pass_on(3, b_left)
    pass_on(1, b_right)

    def far_halves(key, b):
        chunk = chunk_of(a_far, b)
        for way in range(2):
            a_halves[key][way].wait_recv()
            to_sibling(rows_of(chunk, way))

    far_halves(0, at_b)
    pass_on(2, b_far)
    far_halves(3, b_left)
    far_halves(1, b_right)
    far_halves(2, b_far)
    for copy in z_halves + across:
        copy.wait_recv()
    keep.wait()
    keep_view.wait()
    links.drain()


def balance(mesh, one, two, protos, pair):
    nx, ny, nz = mesh.shape["replica"], mesh.shape["batch"] // 2, mesh.shape["proto"]
    segs, width = one.shape
    count = protos.shape[0]
    both = 2 * segs
    z_half = both // nz // 2
    copies = ITERS * (2 * (2 * nx - 1) + (ny - 1) + (nz - 1)) + 80
    hbm = pl.BlockSpec(memory_space=pl.ANY)
    return pl.pallas_call(
        functools.partial(balance_kernel, nx, ny, nz),
        out_shape=(
            jax.ShapeDtypeStruct((both, width), F32),
            jax.ShapeDtypeStruct((count, width), F32),
        ),
        in_specs=[hbm, hbm, hbm, pl.BlockSpec(memory_space=pltpu.VMEM)],
        out_specs=(hbm, hbm),
        scratch_shapes=[
            pltpu.VMEM((both, width), BF16),
            pltpu.VMEM((both, count), F32),
            pltpu.VMEM((both, count), BF16),
            pltpu.VMEM((both, width), BF16),
            pltpu.VMEM((width, both), BF16),
            pltpu.VMEM((segs, width), BF16),
            pltpu.VMEM((count, width), BF16),
            pltpu.VMEM((segs, segs), BF16),
            pltpu.VMEM((both, 128), F32),
            pltpu.VMEM((both, 128), F32),
            pltpu.VMEM((ITERS, 8, 8, 128), F32),
            pltpu.VMEM((ITERS, 8, 8, 128), F32),
            pltpu.VMEM((ITERS, ny, 8, 128), F32),
            pltpu.VMEM((ITERS, 8, 8, 128), F32),
            pltpu.VMEM((ITERS, 16, 128), F32),
            pltpu.VMEM((ITERS, nz, 16, 128), F32),
            pltpu.VMEM((16, 128), F32),
            pltpu.VMEM((count // 128, width, 128), F32),
            pltpu.VMEM((count // 256, width, 128), F32),
            pltpu.VMEM((both, width), F32),
            pltpu.VMEM((128, width), BF16),
            pltpu.VMEM((128, width), F32),
            pltpu.VMEM((both // nz, width), F32),
        ]
        + [pltpu.VMEM((2, 2, width, 128), F32)] * 3
        + [pltpu.VMEM((2, width // 2, 128), F32)] * 3
        + [pltpu.VMEM((2, z_half, width), F32)] * 3
        + [
            pltpu.SemaphoreType.DMA((copies,)),
            pltpu.SemaphoreType.DMA((copies,)),
            pltpu.SemaphoreType.DMA((6,)),
        ],
        compiler_params=pltpu.CompilerParams(
            collective_id=0, has_side_effects=True, vmem_limit_bytes=62 << 20
        ),
        name="balance",
    )(one, two, protos, pair)


def per_device(mesh, view_one, view_two, prototypes, pairing):
    gview, gproto = balance(mesh, view_one, view_two, prototypes, pairing)
    segs = view_one.shape[0]
    return gview[:segs], gview[segs:], gproto


def solution(mesh):
    rows = P(("batch", "replica"), None)
    protos = P("proto", None)
    return jax.shard_map(
        functools.partial(per_device, mesh),
        mesh=mesh,
        in_specs=(rows, rows, protos, rows),
        out_specs=(rows, rows, protos),
        check_vma=False,
    )
```

time: 314 us -> 161 us (0.51)
  waiting for transfers between devices: 163 us -> 0 us
  Pallas kernels: 105 us -> 150 us
  other arithmetic: 19.6 us -> 0 us
  between operations: 14.1 us -> 0.64 us
    psum x2 -> x0, waiting for transfers between devices: 163 us -> none  [the longest x1 119 us: per_device(): dproto = lax.psum(dproto, ('batch', 'replica'))]
    pallas_call x1, Pallas kernels: 105 us -> 150 us  [balance(): pl.pallas_call(functools.partial(balance_kernel, nx, ny, nz), out_shape=(...]
    reduce_sum x5 -> x0, other arithmetic: 11.6 us -> none  [the longest x2 8.16 us: unit_back(): return inv * (grad - unit * jnp.sum(unit * grad, -1, keepdims=True))]
    transpose x1 -> x0, local copies, waits for them, and re-layouts: 9.13 us -> none  [per_device(): dproto = jnp.swapaxes(dproto, 1, 2).reshape(prototypes.shape)]
    mul x2 -> x0, other arithmetic: 7.93 us -> none  [unit_back(): return inv * (grad - unit * jnp.sum(unit * grad, -1, keepdims=True))]
    unnamed x8 -> x1, local copies, waits for them, and re-layouts: 3.17 us -> 7.76 us
  transfers between devices with their start and end apart: 2 -> 0, of which waited for: 2 -> 0; matrix products, arithmetic and copies ran while one was open for 6% -> 0% of each run, Pallas kernels for 0% -> 0%
where the time goes in v2:
time: 161 us
  Pallas kernels  150 us (93%)
  local copies, waits for them, and re-layouts  10.8 us (7%)
    pallas_call x1, Pallas kernels, balance(): pl.pallas_call(functools.partial(balance_kernel, nx, ny, nz), out_shape=(...  150 us
    unnamed x1, local copies, waits for them, and re-layouts  7.76 us

profile of v2, /device:TPU:1, one launch (start us, length us, event | category | flops | bytes accessed | tf_op | source)
XLA Modules:
  0.0 161.2 jit_solution(16710013222288085718)
XLA Ops:
  0.6 149.8 %balance.1 = (f32[1024,512]{1,0:T(8,128)}, f32[4096,512]{1,0:T(8,128)}) custom-call(bf16[512,512]{1,0:T(8,128)(2,1)} %one_hbm.1, bf16[512,512]{1,0:T(8,128)(2,1)} %two_hbm.1, bf16[4096,512]{1,0:T(8,128)(2,1)} %proto_hbm.1, s32[1,512]{1,0:T(1,128)} %pair_ref.1), custom_call_target="tpu_custom_call" | custom-call | tf_op jit(solution)/shard_map/balance/pallas_call | solution.py:494
  150.5 3.0 %fusion = (f32[512,512]{1,0:T(8,128)}, f32[512,512]{1,0:T(8,128)}) fusion(f32[1024,512]{1,0:T(8,128)} %get-tuple-element.5), kind=kLoop, calls=%fused_computation | loop fusion | bytes 4194304 | tf_op jit(solution)/shard_map/slice | solution.py:545
  153.5 7.8 %copy.8 = f32[4096,512]{1,0:T(8,128)} copy(f32[4096,512]{1,0:T(8,128)} %get-tuple-element.14) | data formatting | bytes 16777216

commit v3 on v2

--- a/solution.py
+++ b/solution.py
@@ -60,7 +60,7 @@
     one_hbm, two_hbm, proto_hbm, pair_ref,
     gview_hbm, gproto_hbm,
     raw, expo, dscore, low_seg, low_seg_t, low_two, low_proto, onehot, row_scale, prob_scale,
-    cols, cols_in, cols_y, weight, rows, rows_in, tile_u,
+    cols, cols_in, cols_y, weight, rows, rows_in, tile_u, row_part, tot_part,
     dproto, from_core, dunit, own_proto, gproto, gview,
     a_relay, a_plain, a_joint, b_relay, b_plain, b_joint, z_relay, z_plain, z_joint,
     send_sem, recv_sem, local_sem,
@@ -124,22 +124,18 @@
 
     fetch[0].wait()
     fetch[1].wait()
-    lax.fori_loop(0, segs // 128, norm_views, 0)
+    lax.fori_loop(0, segs // 128, norm_views, 0, unroll=2)
     pair = jnp.broadcast_to(pair_ref[...], (segs, segs))
     number = lax.broadcasted_iota(jnp.int32, (segs, segs), 0)
     onehot[...] = jnp.where(pair == number, 1.0, 0.0).astype(BF16)
     low_seg[segs:both, :] = dot(onehot[...], low_two[...], TN).astype(BF16)
-    for i in range(both // 128):
-        block = low_seg[i * 128:(i + 1) * 128, :].astype(F32)
-        low_seg_t[:, i * 128:(i + 1) * 128] = jnp.transpose(block).astype(BF16)
-
     def norm_protos(i, carry):
         at = pl.ds(pl.multiple_of(i * 128, 128), 128)
         low_proto[at, :] = unit(low_proto[at, :])
         return carry
 
     fetch[2].wait()
-    lax.fori_loop(0, protos // 128, norm_protos, 0)
+    lax.fori_loop(0, protos // 128, norm_protos, 0, unroll=4)
 
     wide = protos // 4
 
@@ -165,21 +161,28 @@
 
             def some(r, acc):
                 acc = list(acc)
-                for t in range(4):
-                    at = pl.ds(pl.multiple_of(first + r * 32 + t * 8, 8), 8)
+                for t in range(16):
+                    at = pl.ds(pl.multiple_of(first + r * 128 + t * 8, 8), 8)
                     u = row_scale[at, :]
                     for l in range(wide // 128):
                         e = expo[at, pl.ds(pl.multiple_of(left + l * 128, 128), 128)]
-                        acc[l] = acc[l] + (e * e) * u
+                        n = (t % 2) * (wide // 128) + l
+                        acc[n] = acc[n] + (e * e) * u
                 return tuple(acc)
 
             zero = jnp.zeros((8, 128), F32)
-            acc = lax.fori_loop(0, segs // 32, some, (zero,) * (wide // 128))
+            acc = lax.fori_loop(0, segs // 128, some, (zero,) * (wide // 64))
+            acc = [acc[l] + acc[wide // 128 + l] for l in range(wide // 128)]
             for l in range(wide // 128):
                 cols[it, k, l:l + 1, :] = jnp.sum(acc[l], axis=0, keepdims=True)
             return carry
 
         lax.fori_loop(0, 8, block, 0)
+
+    def turn_segs():
+        for i in range(both // 128):
+            block = low_seg[i * 128:(i + 1) * 128, :].astype(F32)
+            low_seg_t[:, i * 128:(i + 1) * 128] = jnp.transpose(block).astype(BF16)
 
     def all_cols(it):
         copies = []
@@ -187,6 +190,8 @@
             other, peer = line_peer(s)
             copies.append(links.send(cols.at[it, other], cols_in.at[it, spot], peer))
         cols_in[it, spot] = cols[it, spot]
+        if it == 0:
+            turn_segs()
         for copy in copies:
             copy.wait_recv()
         total = cols_in[it, 0]
@@ -210,30 +215,32 @@
 
     def row_sums(it, with_total):
         def block(b, carry):
-            at = pl.ds(pl.multiple_of(b * 128, 128), 128)
-            view = lax.div(b, 4)
-            acc = jnp.zeros((128, 128), F32)
-            tot = jnp.zeros((128, 128), F32)
+            at = pl.ds(pl.multiple_of(b * 64, 64), 64)
+            view = lax.div(b, segs // 64)
+            acc = jnp.zeros((64, 128), F32)
+            tot = jnp.zeros((64, 128), F32)
             for l in range(protos // 128):
                 e = expo[at, l * 128:(l + 1) * 128]
                 v = weight[it, view * 4 + l // 8, l % 8:l % 8 + 1, :]
                 acc = acc + (e * e) * v
                 if with_total:
                     tot = tot + e
-            rows[it, pl.ds(b, 1), :] = jnp.sum(jnp.transpose(acc), axis=0, keepdims=True)
+            row_part[at, :] = acc
             if with_total:
-                rows[it, pl.ds(8 + b, 1), :] = jnp.sum(jnp.transpose(tot), axis=0, keepdims=True)
+                tot_part[at, :] = tot
             return carry
 
-        lax.fori_loop(0, 8, block, 0)
+        lax.fori_loop(0, both // 64, block, 0)
+        for b in range(both // 128):
+            at = slice(b * 128, (b + 1) * 128)
+            rows[it, b:b + 1, :] = jnp.sum(jnp.transpose(row_part[at, :]), axis=0, keepdims=True)
+            if with_total:
+                rows[it, 8 + b:9 + b, :] = jnp.sum(jnp.transpose(tot_part[at, :]), axis=0, keepdims=True)
 
     def spread(out, row):
-        def block(b, carry):
-            at = pl.ds(pl.multiple_of(b * 128, 128), 128)
-            out[at, :] = jnp.transpose(jnp.broadcast_to(tile_u[pl.ds(row + b, 1), :], (128, 128)))
-            return carry
-
-        lax.fori_loop(0, 8, block, 0)
+        for b in range(both // 128):
+            wide_row = jnp.broadcast_to(tile_u[row + b:row + b + 1, :], (128, 128))
+            out[b * 128:(b + 1) * 128, :] = jnp.transpose(wide_row)
 
     def all_rows(it, with_total, scale):
         size = 16 if with_total else 8
@@ -262,72 +269,85 @@
 
     last = ITERS - 1
 
-    def group(half, a):
-        first_chunk = half * 16 + a * 4
-
-        def grads(j, carry):
-            chunk = first_chunk + j * 2
-            for h in range(2):
-                at = pl.ds(pl.multiple_of((chunk + h) * 128, 128), 128)
-                tile = lax.div(chunk, 8)
-                row = lax.rem(chunk, 8) + h
-                v_one = weight[last, tile, pl.ds(row, 1), :]
-                v_two = weight[last, 4 + tile, pl.ds(row, 1), :]
-                for b in range(segs // 64):
-                    first = slice(b * 64, (b + 1) * 64)
-                    second = slice(segs + b * 64, segs + (b + 1) * 64)
-                    e_one = expo[first, at]
-                    e_two = expo[second, at]
-                    t_one = (e_two * e_two) * row_scale[second, :] * v_two
-                    t_two = (e_one * e_one) * row_scale[first, :] * v_one
-                    dscore[first, at] = (e_one * prob_scale[first, :] - t_one).astype(BF16)
-                    dscore[second, at] = (e_two * prob_scale[second, :] - t_two).astype(BF16)
-            at = pl.ds(pl.multiple_of(chunk * 128, 256), 256)
-            part = dot(low_seg_t[...], dscore[:, at], NN)
-            dproto[chunk] = part[:, 0:128]
-            dproto[chunk + 1] = part[:, 128:256]
+    half_b = 256
+
+    def elements(ds, chunk, j):
+        for h in range(2):
+            at = pl.ds(pl.multiple_of((chunk + j * 2 + h) * 128, 128), 128)
+            to = pl.ds(pl.multiple_of(j * half_b + h * 128, 128), 128)
+            tile = lax.div(chunk, 8)
+            row = lax.rem(chunk, 8) + j * 2 + h
+            v_one = weight[last, tile, pl.ds(row, 1), :]
+            v_two = weight[last, 4 + tile, pl.ds(row, 1), :]
+            for b in range(segs // 64):
+                first = slice(b * 64, (b + 1) * 64)
+                second = slice(segs + b * 64, segs + (b + 1) * 64)
+                e_one = expo[first, at]
+                e_two = expo[second, at]
+                t_one = (e_two * e_two) * row_scale[second, :] * v_two
+                t_two = (e_one * e_one) * row_scale[first, :] * v_one
+                ds[first, to] = (e_one * prob_scale[first, :] - t_one).astype(BF16)
+                ds[second, to] = (e_two * prob_scale[second, :] - t_two).astype(BF16)
+
+    def step(new, old):
+        def both_parts(j, carry):
+            if old is not None:
+                at = pl.ds(pl.multiple_of(j * half_b, half_b), half_b)
+                part = dot(low_seg_t[...], dscore[old][:, at], NN)
+                dproto[old][2 * j] = part[:, 0:128]
+                dproto[old][2 * j + 1] = part[:, 128:256]
+            if new is not None:
+                elements(dscore[new], chunks[new], j)
             return carry
 
-        lax.fori_loop(0, 2, grads, 0)
-        return first_chunk
+        lax.fori_loop(0, 2, both_parts, 0)
 
     order = (2, 1, 3, 0)
-    crossing = []
+    chunks, spots = [], []
     for t in order:
-        a = lax.rem(at_b + t, 4)
-        first = group(1 - core, a)
-        crossing.append(links.send(dproto.at[pl.ds(first, 4)], from_core.at[pl.ds(a * 4, 4)], sibling))
+        for half, place in ((1 - core, at_b), (core, at_a)):
+            spots.append(lax.rem(place + t, 4))
+            chunks.append(half * 16 + spots[-1] * 4)
     relays, plains, joints = [None] * 2, [None] * 2, [None] * 2
-    base = {}
-    for t, arrival in zip(order, crossing):
-        a = lax.rem(at_a + t, 4)
-        first = group(core, a)
-        base[t] = first
-        arrival.wait_recv()
+    crossing = [None] * 8
+    step(0, None)
+    for g in range(8):
+        step(g + 1 if g < 7 else None, g)
+        if g % 2 == 0:
+            crossing[g] = links.send(dproto[g], from_core.at[g // 2], sibling)
+            continue
+        crossing[g - 1].wait_recv()
         for q in range(4):
-            dproto[first + q] = dproto[first + q] + from_core[a * 4 + q]
-        low, high = dproto.at[pl.ds(first, 2)], dproto.at[pl.ds(first + 2, 2)]
+            dproto[g][q] = dproto[g][q] + from_core[g // 2, q]
+        low, high = dproto[g].at[0:2], dproto[g].at[2:4]
+        t = order[g // 2]
         if t == 2:
             relays = [links.send(low, a_relay.at[0], a_peer(1)), links.send(high, a_relay.at[1], a_peer(3))]
         if t == 1:
             plains[0] = links.send(high, a_plain.at[0], a_peer(1))
         if t == 3:
             plains[1] = links.send(low, a_plain.at[1], a_peer(3))
+    d_right, d_left, d_own = dproto[3], dproto[5], dproto[7]
 
     def views(i):
         at = slice(i * 256, (i + 1) * 256)
-        dunit[at, :] = dot(dscore[at, :], low_proto[...], NN)
+        total = None
+        for g in range(8):
+            rows_g = low_proto[pl.ds(pl.multiple_of(chunks[g] * 128, 512), 512), :]
+            term = dot(dscore[g][at, :], rows_g, NN)
+            total = term if total is None else total + term
+        dunit[at, :] = total
 
     views(0)
     views(1)
     relays[0].wait_recv()
     for q in range(2):
-        dproto[base[1] + q] = dproto[base[1] + q] + a_relay[0, q]
-    joints[0] = links.send(dproto.at[pl.ds(base[1], 2)], a_joint.at[0], a_peer(1))
+        d_right[q] = d_right[q] + a_relay[0, q]
+    joints[0] = links.send(d_right.at[0:2], a_joint.at[0], a_peer(1))
     relays[1].wait_recv()
     for q in range(2):
-        dproto[base[3] + 2 + q] = dproto[base[3] + 2 + q] + a_relay[1, q]
-    joints[1] = links.send(dproto.at[pl.ds(base[3] + 2, 2)], a_joint.at[1], a_peer(3))
+        d_left[2 + q] = d_left[2 + q] + a_relay[1, q]
+    joints[1] = links.send(d_left.at[2:4], a_joint.at[1], a_peer(3))
 
     views(2)
     views(3)
@@ -355,21 +375,20 @@
         links.send(part(dunit, z_left, seg_part, True), z_plain.at[1], z_peer(3)),
     ]
 
-    own = base[0]
     for copy in plains + joints:
         copy.wait_recv()
     for q in range(2):
-        dproto[own + q] = dproto[own + q] + (a_joint[0, q] + a_plain[1, q])
-        dproto[own + 2 + q] = dproto[own + 2 + q] + (a_plain[0, q] + a_joint[1, q])
+        d_own[q] = d_own[q] + (a_joint[0, q] + a_plain[1, q])
+        d_own[2 + q] = d_own[2 + q] + (a_plain[0, q] + a_joint[1, q])
     b_right, b_left, b_far = lax.rem(at_b + 1, 4), lax.rem(at_b + 3, 4), lax.rem(at_b + 2, 4)
     half = width // 2
     b_relays = [
-        links.send(dproto.at[own + b_far, 0:half], b_relay.at[0], b_peer(1)),
-        links.send(dproto.at[own + b_far, half:width], b_relay.at[1], b_peer(3)),
+        links.send(d_own.at[b_far, 0:half], b_relay.at[0], b_peer(1)),
+        links.send(d_own.at[b_far, half:width], b_relay.at[1], b_peer(3)),
     ]
     b_plains = [
-        links.send(dproto.at[own + b_right, half:width], b_plain.at[0], b_peer(1)),
-        links.send(dproto.at[own + b_left, 0:half], b_plain.at[1], b_peer(3)),
+        links.send(d_own.at[b_right, half:width], b_plain.at[0], b_peer(1)),
+        links.send(d_own.at[b_left, 0:half], b_plain.at[1], b_peer(3)),
     ]
 
     z_half = seg_part // 2
@@ -384,15 +403,15 @@
     for way, k, skip, peer in ((0, b_right, 0, b_peer(1)), (1, b_left, half, b_peer(3))):
         b_relays[way].wait_recv()
         at = slice(skip, skip + half)
-        dproto[own + k, at, :] = dproto[own + k, at, :] + b_relay[way]
-        b_joints.append(links.send(dproto.at[own + k, at], b_joint.at[way], peer))
+        d_own[k, at, :] = d_own[k, at, :] + b_relay[way]
+        b_joints.append(links.send(d_own.at[k, at], b_joint.at[way], peer))
     for copy in b_plains + b_joints:
         copy.wait_recv()
-    me = own + at_b
-    dproto[me, 0:half, :] = dproto[me, 0:half, :] + (b_joint[0] + b_plain[1])
-    dproto[me, half:width, :] = dproto[me, half:width, :] + (b_plain[0] + b_joint[1])
+    me = at_b
+    d_own[me, 0:half, :] = d_own[me, 0:half, :] + (b_joint[0] + b_plain[1])
+    d_own[me, half:width, :] = d_own[me, half:width, :] + (b_plain[0] + b_joint[1])
     fetch[3].wait()
-    gproto[...] = back(jnp.transpose(dproto[me]), own_proto[...])
+    gproto[...] = back(jnp.transpose(d_own[me]), own_proto[...])
 
     def rows_of(chunk, part=None):
         if part is None:
@@ -502,7 +521,7 @@
         scratch_shapes=[
             pltpu.VMEM((both, width), BF16),
             pltpu.VMEM((both, count), F32),
-            pltpu.VMEM((both, count), BF16),
+            [pltpu.VMEM((both, count // 8), BF16)] * 8,
             pltpu.VMEM((both, width), BF16),
             pltpu.VMEM((width, both), BF16),
             pltpu.VMEM((segs, width), BF16),
@@ -517,8 +536,10 @@
             pltpu.VMEM((ITERS, 16, 128), F32),
             pltpu.VMEM((ITERS, nz, 16, 128), F32),
             pltpu.VMEM((16, 128), F32),
-            pltpu.VMEM((count // 128, width, 128), F32),
-            pltpu.VMEM((count // 256, width, 128), F32),
+            pltpu.VMEM((both, 128), F32),
+            pltpu.VMEM((both, 128), F32),
+            [pltpu.VMEM((4, width, 128), F32)] * 8,
+            pltpu.VMEM((4, 4, width, 128), F32),
             pltpu.VMEM((both, width), F32),
             pltpu.VMEM((128, width), BF16),
             pltpu.VMEM((128, width), F32),
@@ -539,10 +560,38 @@
     )(one, two, protos, pair)
 
 
+def hand_over_kernel(gview, gproto, one_out, two_out, proto_out, sems):
+    segs = one_out.shape[0]
+    parts = sems.shape[0] - 2
+    rows = proto_out.shape[0] // parts
+    copies = [
+        pltpu.make_async_copy(gproto.at[i * rows:(i + 1) * rows], proto_out.at[i * rows:(i + 1) * rows], sems.at[i])
+        for i in range(parts)
+    ]
+    copies.append(pltpu.make_async_copy(gview.at[0:segs], one_out, sems.at[parts]))
+    copies.append(pltpu.make_async_copy(gview.at[segs:2 * segs], two_out, sems.at[parts + 1]))
+    for copy in copies:
+        copy.start()
+    for copy in copies:
+        copy.wait()
+
+
+def hand_over(gview, gproto):
+    half = jax.ShapeDtypeStruct((gview.shape[0] // 2, gview.shape[1]), F32)
+    hbm = pl.BlockSpec(memory_space=pl.ANY)
+    return pl.pallas_call(
+        hand_over_kernel,
+        out_shape=(half, half, jax.ShapeDtypeStruct(gproto.shape, F32)),
+        in_specs=[hbm] * 2,
+        out_specs=(hbm,) * 3,
+        scratch_shapes=[pltpu.SemaphoreType.DMA((10,))],
+        name="hand_over",
+    )(gview, gproto)
+
+
 def per_device(mesh, view_one, view_two, prototypes, pairing):
     gview, gproto = balance(mesh, view_one, view_two, prototypes, pairing)
-    segs = view_one.shape[0]
-    return gview[:segs], gview[segs:], gproto
+    return hand_over(gview, gproto)
 
 
 def solution(mesh):

time: 161 us -> 465 us (2.89)
  Pallas kernels: 150 us -> 464 us
  local copies, waits for them, and re-layouts: 10.8 us -> 0 us
    pallas_call x0 -> x1, Pallas kernels: none -> 319 us  [hand_over(): pl.pallas_call(hand_over_kernel, out_shape=(half, half, jax.ShapeDtypeStr...]
    unnamed x1 -> x0, local copies, waits for them, and re-layouts: 7.76 us -> none
where the time goes in v3:
time: 465 us
  Pallas kernels  464 us (100%)
    pallas_call x1, Pallas kernels, hand_over(): pl.pallas_call(hand_over_kernel, out_shape=(half, half, jax.ShapeDtypeStr...  319 us
    pallas_call x1, Pallas kernels, balance(): pl.pallas_call(functools.partial(balance_kernel, nx, ny, nz), out_shape=(...  145 us

profile of v3, /device:TPU:1, one launch (start us, length us, event | category | flops | bytes accessed | tf_op | source)
XLA Modules:
  0.0 465.0 jit_solution(8673295196151137568)
XLA Ops:
  0.6 145.4 %balance.1 = (f32[1024,512]{1,0:T(8,128)}, f32[4096,512]{1,0:T(8,128)}) custom-call(bf16[512,512]{1,0:T(8,128)(2,1)} %one_hbm.1, bf16[512,512]{1,0:T(8,128)(2,1)} %two_hbm.1, bf16[4096,512]{1,0:T(8,128)(2,1)} %proto_hbm.1, s32[1,512]{1,0:T(1,128)} %pair_ref.1), custom_call_target="tpu_custom_call" | custom-call | tf_op jit(solution)/shard_map/balance/pallas_call | solution.py:513
  146.0 318.8 %hand_over.1 = (f32[512,512]{1,0:T(8,128)}, f32[512,512]{1,0:T(8,128)}, f32[4096,512]{1,0:T(8,128)}) custom-call(f32[1024,512]{1,0:T(8,128)} %get-tuple-element.5.gview, f32[4096,512]{1,0:T(8,128)} %get-tuple-element.6.gproto), custom_call_target="tpu_custom_call" | custom-call | tf_op jit(solution)/shard_map/hand_over/pallas_call | solution.py:582

commit v4 on v3

--- a/solution.py
+++ b/solution.py
@@ -161,11 +161,13 @@
 
             def some(r, acc):
                 acc = list(acc)
+                at = pl.ds(pl.multiple_of(first + r * 128, 128), 128)
+                scale = row_scale.at[at]
+                tiles = expo.at[at, pl.ds(pl.multiple_of(left, 128), wide)]
                 for t in range(16):
-                    at = pl.ds(pl.multiple_of(first + r * 128 + t * 8, 8), 8)
-                    u = row_scale[at, :]
+                    u = scale[t * 8:(t + 1) * 8, :]
                     for l in range(wide // 128):
-                        e = expo[at, pl.ds(pl.multiple_of(left + l * 128, 128), 128)]
+                        e = tiles[t * 8:(t + 1) * 8, l * 128:(l + 1) * 128]
                         n = (t % 2) * (wide // 128) + l
                         acc[n] = acc[n] + (e * e) * u
                 return tuple(acc)
@@ -219,9 +221,11 @@
             view = lax.div(b, segs // 64)
             acc = jnp.zeros((64, 128), F32)
             tot = jnp.zeros((64, 128), F32)
+            tiles = expo.at[at]
+            scale = weight.at[it, pl.ds(view * 4, 4)]
             for l in range(protos // 128):
-                e = expo[at, l * 128:(l + 1) * 128]
-                v = weight[it, view * 4 + l // 8, l % 8:l % 8 + 1, :]
+                e = tiles[:, l * 128:(l + 1) * 128]
+                v = scale[l // 8, l % 8:l % 8 + 1, :]
                 acc = acc + (e * e) * v
                 if with_total:
                     tot = tot + e
@@ -272,22 +276,25 @@
     half_b = 256
 
     def elements(ds, chunk, j):
-        for h in range(2):
-            at = pl.ds(pl.multiple_of((chunk + j * 2 + h) * 128, 128), 128)
-            to = pl.ds(pl.multiple_of(j * half_b + h * 128, 128), 128)
-            tile = lax.div(chunk, 8)
-            row = lax.rem(chunk, 8) + j * 2 + h
-            v_one = weight[last, tile, pl.ds(row, 1), :]
-            v_two = weight[last, 4 + tile, pl.ds(row, 1), :]
-            for b in range(segs // 64):
-                first = slice(b * 64, (b + 1) * 64)
-                second = slice(segs + b * 64, segs + (b + 1) * 64)
-                e_one = expo[first, at]
-                e_two = expo[second, at]
-                t_one = (e_two * e_two) * row_scale[second, :] * v_two
-                t_two = (e_one * e_one) * row_scale[first, :] * v_one
-                ds[first, to] = (e_one * prob_scale[first, :] - t_one).astype(BF16)
-                ds[second, to] = (e_two * prob_scale[second, :] - t_two).astype(BF16)
+        tiles = expo.at[:, pl.ds(pl.multiple_of(chunk * 128 + j * half_b, half_b), half_b)]
+        to = ds.at[:, pl.ds(pl.multiple_of(j * half_b, half_b), half_b)]
+        tile = lax.div(chunk, 8)
+        row = lax.rem(chunk, 8) + j * 2
+        v_one = [weight[last, tile, pl.ds(row + h, 1), :] for h in range(2)]
+        v_two = [weight[last, 4 + tile, pl.ds(row + h, 1), :] for h in range(2)]
+        for b in range(segs // 32):
+            first = slice(b * 32, (b + 1) * 32)
+            second = slice(segs + b * 32, segs + (b + 1) * 32)
+            u_one, u_two = row_scale[first, :], row_scale[second, :]
+            p_one, p_two = prob_scale[first, :], prob_scale[second, :]
+            for h in range(2):
+                at = slice(h * 128, (h + 1) * 128)
+                e_one = tiles[first, at]
+                e_two = tiles[second, at]
+                t_one = (e_two * e_two) * u_two * v_two[h]
+                t_two = (e_one * e_one) * u_one * v_one[h]
+                to[first, at] = (e_one * p_one - t_one).astype(BF16)
+                to[second, at] = (e_two * p_two - t_two).astype(BF16)
 
     def step(new, old):
         def both_parts(j, carry):
@@ -560,31 +567,35 @@
     )(one, two, protos, pair)
 
 
-def hand_over_kernel(gview, gproto, one_out, two_out, proto_out, sems):
-    segs = one_out.shape[0]
-    parts = sems.shape[0] - 2
-    rows = proto_out.shape[0] // parts
-    copies = [
-        pltpu.make_async_copy(gproto.at[i * rows:(i + 1) * rows], proto_out.at[i * rows:(i + 1) * rows], sems.at[i])
-        for i in range(parts)
-    ]
-    copies.append(pltpu.make_async_copy(gview.at[0:segs], one_out, sems.at[parts]))
-    copies.append(pltpu.make_async_copy(gview.at[segs:2 * segs], two_out, sems.at[parts + 1]))
-    for copy in copies:
+def hand_over_kernel(gview, gproto, one_out, two_out, proto_out, stage, sems):
+    size = stage.shape[1]
+    pairs = [(gview.at[0:size], one_out), (gview.at[size:2 * size], two_out)]
+    for i in range(proto_out.shape[0] // size):
+        at = slice(i * size, (i + 1) * size)
+        pairs.append((gproto.at[at], proto_out.at[at]))
+    come = [pltpu.make_async_copy(src, stage.at[i], sems.at[0, i]) for i, (src, _) in enumerate(pairs)]
+    go = [pltpu.make_async_copy(stage.at[i], dst, sems.at[1, i]) for i, (_, dst) in enumerate(pairs)]
+    for copy in come:
         copy.start()
-    for copy in copies:
+    for arrived, copy in zip(come, go):
+        arrived.wait()
+        copy.start()
+    for copy in go:
         copy.wait()
 
 
 def hand_over(gview, gproto):
-    half = jax.ShapeDtypeStruct((gview.shape[0] // 2, gview.shape[1]), F32)
-    hbm = pl.BlockSpec(memory_space=pl.ANY)
+    segs, width = gview.shape[0] // 2, gview.shape[1]
+    half = jax.ShapeDtypeStruct((segs, width), F32)
+    parts = 2 + gproto.shape[0] // segs
+    hbm = pl.BlockSpec(memory_space=pltpu.HBM)
     return pl.pallas_call(
         hand_over_kernel,
         out_shape=(half, half, jax.ShapeDtypeStruct(gproto.shape, F32)),
         in_specs=[hbm] * 2,
         out_specs=(hbm,) * 3,
-        scratch_shapes=[pltpu.SemaphoreType.DMA((10,))],
+        scratch_shapes=[pltpu.VMEM((parts, segs, width), F32), pltpu.SemaphoreType.DMA((2, parts))],
+        compiler_params=pltpu.CompilerParams(vmem_limit_bytes=62 << 20),
         name="hand_over",
     )(gview, gproto)
 

time: 465 us -> 147 us (0.32)
  Pallas kernels: 464 us -> 146 us
    pallas_call x1, Pallas kernels: 319 us -> 8.19 us  [hand_over(): pl.pallas_call(hand_over_kernel, out_shape=(half, half, jax.ShapeDtypeStr...]
    pallas_call x1, Pallas kernels: 145 us -> 138 us  [balance(): pl.pallas_call(functools.partial(balance_kernel, nx, ny, nz), out_shape=(...]
where the time goes in v4:
time: 147 us
  Pallas kernels  146 us (99%)
    pallas_call x1, Pallas kernels, balance(): pl.pallas_call(functools.partial(balance_kernel, nx, ny, nz), out_shape=(...  138 us
    pallas_call x1, Pallas kernels, hand_over(): pl.pallas_call(hand_over_kernel, out_shape=(half, half, jax.ShapeDtypeStr...  8.19 us

profile of v4, /device:TPU:1, one launch (start us, length us, event | category | flops | bytes accessed | tf_op | source)
XLA Modules:
  0.0 146.7 jit_solution(15701075652386610011)
XLA Ops:
  0.6 137.7 %balance.1 = (f32[1024,512]{1,0:T(8,128)}, f32[4096,512]{1,0:T(8,128)}) custom-call(bf16[512,512]{1,0:T(8,128)(2,1)} %one_hbm.1, bf16[512,512]{1,0:T(8,128)(2,1)} %two_hbm.1, bf16[4096,512]{1,0:T(8,128)(2,1)} %proto_hbm.1, s32[1,512]{1,0:T(1,128)} %pair_ref.1), custom_call_target="tpu_custom_call" | custom-call | tf_op jit(solution)/shard_map/balance/pallas_call | solution.py:520
  138.4 8.2 %hand_over.1 = (f32[512,512]{1,0:T(8,128)}, f32[512,512]{1,0:T(8,128)}, f32[4096,512]{1,0:T(8,128)}) custom-call(f32[1024,512]{1,0:T(8,128)} %get-tuple-element.5.gview, f32[4096,512]{1,0:T(8,128)} %get-tuple-element.6.gproto), custom_call_target="tpu_custom_call" | custom-call | tf_op jit(solution)/shard_map/hand_over/pallas_call | solution.py:592

commit v5 on v4

--- a/solution.py
+++ b/solution.py
@@ -60,25 +60,20 @@
     one_hbm, two_hbm, proto_hbm, pair_ref,
     gview_hbm, gproto_hbm,
     raw, expo, dscore, low_seg, low_seg_t, low_two, low_proto, onehot, row_scale, prob_scale,
-    cols, cols_in, cols_y, weight, rows, rows_in, tile_u, row_part, tot_part,
+    cols, cols_in, plane_in, weight, rows, rows_in, tile_u, row_part, tot_part,
     dproto, from_core, dunit, own_proto, gproto, gview,
     a_relay, a_plain, a_joint, b_relay, b_plain, b_joint, z_relay, z_plain, z_joint,
     send_sem, recv_sem, local_sem,
 ):
     y, core, x, z = here()
-    line = 2 * nx
-    spot = core * nx + x
+    spot = y * nx + x
     links = Links(send_sem, recv_sem)
     at_a = core * y + (1 - core) * x
     at_b = core * x + (1 - core) * y
     mine = core * 16 + at_a * 4 + at_b
 
-    def line_peer(step):
-        other = lax.rem(spot + step, line)
-        return other, (y * 2 + lax.div(other, nx), lax.rem(other, nx), z)
-
-    def y_peer(step):
-        return (lax.rem(y + step, ny) * 2 + core, x, z)
+    def plane_peer(dx, dy):
+        return (lax.rem(y + dy, ny) * 2 + core, lax.rem(x + dx, nx), z)
 
     def z_peer(step):
         return (y * 2 + core, x, lax.rem(z + step, nz))
@@ -94,19 +89,26 @@
     segs = one_hbm.shape[0]
     protos, width = low_proto.shape
     both = 2 * segs
+    pieces = 8
+    piece = protos // pieces
     fetch = [
         pltpu.make_async_copy(one_hbm, raw.at[0:segs], local_sem.at[0]),
         pltpu.make_async_copy(two_hbm, raw.at[segs:both], local_sem.at[1]),
-        pltpu.make_async_copy(proto_hbm, low_proto, local_sem.at[2]),
-        pltpu.make_async_copy(proto_hbm.at[pl.ds(mine * 128, 128)], own_proto, local_sem.at[3]),
+        pltpu.make_async_copy(proto_hbm.at[pl.ds(mine * 128, 128)], own_proto, local_sem.at[2]),
     ]
-    for copy in fetch:
+    fetch_protos = [
+        pltpu.make_async_copy(
+            proto_hbm.at[i * piece:(i + 1) * piece], low_proto.at[i * piece:(i + 1) * piece], local_sem.at[3 + i]
+        )
+        for i in range(pieces)
+    ]
+    for copy in fetch + fetch_protos:
         copy.start()
-    peers = (
-        [line_peer(s)[1] for s in range(1, line)]
-        + [y_peer(s) for s in range(1, ny)]
-        + [z_peer(s) for s in range(1, nz)]
-    )
+    def hops(step):
+        return min(step[0], nx - step[0]) + min(step[1], ny - step[1])
+
+    steps = sorted([(dx, dy) for dx in range(nx) for dy in range(ny)][1:], key=hops, reverse=True)
+    peers = [plane_peer(*p) for p in steps] + [z_peer(s) for s in range(1, nz)] + [sibling]
     barrier = pltpu.get_barrier_semaphore()
     for peer in peers:
         pl.semaphore_signal(barrier, inc=1, device_id=peer, device_id_type=MESH)
@@ -134,8 +136,9 @@
         low_proto[at, :] = unit(low_proto[at, :])
         return carry
 
-    fetch[2].wait()
-    lax.fori_loop(0, protos // 128, norm_protos, 0, unroll=4)
+    for i, copy in enumerate(fetch_protos):
+        copy.wait()
+        lax.fori_loop(i * piece // 128, (i + 1) * piece // 128, norm_protos, 0, unroll=4)
 
     wide = protos // 4
 
@@ -154,8 +157,9 @@
 
     lax.fori_loop(0, 4, scores, 0)
 
-    def col_sums(it):
-        def block(k, carry):
+    def col_sums(it, view):
+        def block(j, carry):
+            k = view * 4 + j
             first = pl.multiple_of(lax.div(k, 4) * segs, segs)
             left = lax.rem(k, 4) * wide
 
@@ -179,46 +183,38 @@
                 cols[it, k, l:l + 1, :] = jnp.sum(acc[l], axis=0, keepdims=True)
             return carry
 
-        lax.fori_loop(0, 8, block, 0)
+        lax.fori_loop(0, 4, block, 0)
 
     def turn_segs():
         for i in range(both // 128):
             block = low_seg[i * 128:(i + 1) * 128, :].astype(F32)
             low_seg_t[:, i * 128:(i + 1) * 128] = jnp.transpose(block).astype(BF16)
 
-    def all_cols(it):
-        copies = []
-        for s in range(1, line):
-            other, peer = line_peer(s)
-            copies.append(links.send(cols.at[it, other], cols_in.at[it, spot], peer))
-        cols_in[it, spot] = cols[it, spot]
+    def tiles_of(k):
+        return pl.ds(pl.multiple_of(k * 4, 4), 4)
+
+    def swap_cols(it):
+        return links.send(cols.at[it, tiles_of(1 - core)], cols_in.at[it], sibling)
+
+    def all_cols(it, swap):
+        swap.wait_recv()
+        plane_in[it, spot] = cols[it, tiles_of(core)] + cols_in[it]
+        copies = [
+            links.send(plane_in.at[it, spot], plane_in.at[it, spot], plane_peer(*p)) for p in steps
+        ]
         if it == 0:
             turn_segs()
         for copy in copies:
             copy.wait_recv()
-        total = cols_in[it, 0]
-        for k in range(1, line):
-            total = total + cols_in[it, k]
-        cols_y[it, y] = total
-        copies = []
-        for s in range(1, ny):
-            copies.append(links.send(cols_y.at[it, y], cols_y.at[it, y], y_peer(s)))
-        for copy in copies:
-            copy.wait_recv()
-        total = cols_y[it, 0]
-        for k in range(1, ny):
-            total = total + cols_y[it, k]
-        weight[it, spot] = 1.0 / total
-        copies = []
-        for s in range(1, line):
-            copies.append(links.send(weight.at[it, spot], weight.at[it, spot], line_peer(s)[1]))
-        for copy in copies:
-            copy.wait_recv()
-
-    def row_sums(it, with_total):
+        total = plane_in[it, 0]
+        for k in range(1, nx * ny):
+            total = total + plane_in[it, k]
+        weight[it, tiles_of(core)] = 1.0 / total
+        return links.send(weight.at[it, tiles_of(core)], weight.at[it, tiles_of(core)], sibling)
+
+    def row_sums(it, with_total, view):
         def block(b, carry):
-            at = pl.ds(pl.multiple_of(b * 64, 64), 64)
-            view = lax.div(b, segs // 64)
+            at = pl.ds(pl.multiple_of(view * segs + b * 64, 64), 64)
             acc = jnp.zeros((64, 128), F32)
             tot = jnp.zeros((64, 128), F32)
             tiles = expo.at[at]
@@ -234,7 +230,9 @@
                 tot_part[at, :] = tot
             return carry
 
-        lax.fori_loop(0, both // 64, block, 0)
+        lax.fori_loop(0, segs // 64, block, 0)
+
+    def turn_sums(it, with_total):
         for b in range(both // 128):
             at = slice(b * 128, (b + 1) * 128)
             rows[it, b:b + 1, :] = jnp.sum(jnp.transpose(row_part[at, :]), axis=0, keepdims=True)
@@ -266,9 +264,16 @@
     pl.semaphore_wait(barrier, len(peers))
     for it in range(ITERS):
         if it:
-            col_sums(it)
-        all_cols(it)
-        row_sums(it, it == 0)
+            col_sums(it, 1 - core)
+            swap = swap_cols(it)
+            col_sums(it, core)
+        else:
+            swap = swap_cols(it)
+        back_copy = all_cols(it, swap)
+        row_sums(it, it == 0, core)
+        back_copy.wait_recv()
+        row_sums(it, it == 0, 1 - core)
+        turn_sums(it, it == 0)
         all_rows(it, it == 0, 5.0 if it == ITERS - 1 else 1.0)
 
     last = ITERS - 1
@@ -388,14 +393,14 @@
         d_own[q] = d_own[q] + (a_joint[0, q] + a_plain[1, q])
         d_own[2 + q] = d_own[2 + q] + (a_plain[0, q] + a_joint[1, q])
     b_right, b_left, b_far = lax.rem(at_b + 1, 4), lax.rem(at_b + 3, 4), lax.rem(at_b + 2, 4)
-    half = width // 2
+    width_half = width // 2
     b_relays = [
-        links.send(d_own.at[b_far, 0:half], b_relay.at[0], b_peer(1)),
-        links.send(d_own.at[b_far, half:width], b_relay.at[1], b_peer(3)),
+        links.send(d_own.at[b_far, 0:width_half], b_relay.at[0], b_peer(1)),
+        links.send(d_own.at[b_far, width_half:width], b_relay.at[1], b_peer(3)),
     ]
     b_plains = [
-        links.send(d_own.at[b_right, half:width], b_plain.at[0], b_peer(1)),
-        links.send(d_own.at[b_left, 0:half], b_plain.at[1], b_peer(3)),
+        links.send(d_own.at[b_right, width_half:width], b_plain.at[0], b_peer(1)),
+        links.send(d_own.at[b_left, 0:width_half], b_plain.at[1], b_peer(3)),
     ]
 
     z_half = seg_part // 2
@@ -407,17 +412,17 @@
         z_joints.append(links.send(dunit.at[at], z_joint.at[way], peer))
 
     b_joints = []
-    for way, k, skip, peer in ((0, b_right, 0, b_peer(1)), (1, b_left, half, b_peer(3))):
+    for way, k, skip, peer in ((0, b_right, 0, b_peer(1)), (1, b_left, width_half, b_peer(3))):
         b_relays[way].wait_recv()
-        at = slice(skip, skip + half)
+        at = slice(skip, skip + width_half)
         d_own[k, at, :] = d_own[k, at, :] + b_relay[way]
         b_joints.append(links.send(d_own.at[k, at], b_joint.at[way], peer))
     for copy in b_plains + b_joints:
         copy.wait_recv()
     me = at_b
-    d_own[me, 0:half, :] = d_own[me, 0:half, :] + (b_joint[0] + b_plain[1])
-    d_own[me, half:width, :] = d_own[me, half:width, :] + (b_plain[0] + b_joint[1])
-    fetch[3].wait()
+    d_own[me, 0:width_half, :] = d_own[me, 0:width_half, :] + (b_joint[0] + b_plain[1])
+    d_own[me, width_half:width, :] = d_own[me, width_half:width, :] + (b_plain[0] + b_joint[1])
+    fetch[2].wait()
     gproto[...] = back(jnp.transpose(d_own[me]), own_proto[...])
 
     def rows_of(chunk, part=None):
@@ -436,7 +441,7 @@
     b_whole = [links.send(gproto, rows_of(mine), b_peer(1)), links.send(gproto, rows_of(mine), b_peer(3))]
     a_whole = {0: [links.send(gproto, rows_of(mine), a_peer(1)), links.send(gproto, rows_of(mine), a_peer(3))]}
     to_sibling(rows_of(mine), gproto)
-    keep = pltpu.make_async_copy(gproto, rows_of(mine), local_sem.at[4])
+    keep = pltpu.make_async_copy(gproto, rows_of(mine), local_sem.at[11])
     keep.start()
 
     for copy in z_plains + z_joints:
@@ -449,7 +454,7 @@
     gview[...] = back(dunit[at, :], raw[at, :])
     place = gview_hbm.at[at]
     z_whole = [links.send(gview, place, z_peer(1)), links.send(gview, place, z_peer(3))]
-    keep_view = pltpu.make_async_copy(gview, place, local_sem.at[5])
+    keep_view = pltpu.make_async_copy(gview, place, local_sem.at[12])
     keep_view.start()
 
     b_halves, a_halves = [], {}
@@ -515,7 +520,7 @@
     count = protos.shape[0]
     both = 2 * segs
     z_half = both // nz // 2
-    copies = ITERS * (2 * (2 * nx - 1) + (ny - 1) + (nz - 1)) + 80
+    copies = ITERS * (nx * ny + nz + 1) + 80
     hbm = pl.BlockSpec(memory_space=pl.ANY)
     return pl.pallas_call(
         functools.partial(balance_kernel, nx, ny, nz),
@@ -537,8 +542,8 @@
             pltpu.VMEM((both, 128), F32),
             pltpu.VMEM((both, 128), F32),
             pltpu.VMEM((ITERS, 8, 8, 128), F32),
-            pltpu.VMEM((ITERS, 8, 8, 128), F32),
-            pltpu.VMEM((ITERS, ny, 8, 128), F32),
+            pltpu.VMEM((ITERS, 4, 8, 128), F32),
+            pltpu.VMEM((ITERS, nx * ny, 4, 8, 128), F32),
             pltpu.VMEM((ITERS, 8, 8, 128), F32),
             pltpu.VMEM((ITERS, 16, 128), F32),
             pltpu.VMEM((ITERS, nz, 16, 128), F32),
@@ -558,7 +563,7 @@
         + [
             pltpu.SemaphoreType.DMA((copies,)),
             pltpu.SemaphoreType.DMA((copies,)),
-            pltpu.SemaphoreType.DMA((6,)),
+            pltpu.SemaphoreType.DMA((13,)),
         ],
         compiler_params=pltpu.CompilerParams(
             collective_id=0, has_side_effects=True, vmem_limit_bytes=62 << 20
@@ -569,17 +574,25 @@
 
 def hand_over_kernel(gview, gproto, one_out, two_out, proto_out, stage, sems):
     size = stage.shape[1]
-    pairs = [(gview.at[0:size], one_out), (gview.at[size:2 * size], two_out)]
+    pairs = []
+    for i in range(one_out.shape[0] // size):
+        at = slice(i * size, (i + 1) * size)
+        pairs.append((gview.at[at], one_out.at[at]))
+        late = slice(one_out.shape[0] + i * size, one_out.shape[0] + (i + 1) * size)
+        pairs.append((gview.at[late], two_out.at[at]))
     for i in range(proto_out.shape[0] // size):
         at = slice(i * size, (i + 1) * size)
         pairs.append((gproto.at[at], proto_out.at[at]))
     come = [pltpu.make_async_copy(src, stage.at[i], sems.at[0, i]) for i, (src, _) in enumerate(pairs)]
     go = [pltpu.make_async_copy(stage.at[i], dst, sems.at[1, i]) for i, (_, dst) in enumerate(pairs)]
-    for copy in come:
+    ahead = 4
+    for copy in come[:ahead]:
         copy.start()
-    for arrived, copy in zip(come, go):
-        arrived.wait()
+    for i, copy in enumerate(go):
+        come[i].wait()
         copy.start()
+        if i + ahead < len(come):
+            come[i + ahead].start()
     for copy in go:
         copy.wait()
 
@@ -587,14 +600,15 @@
 def hand_over(gview, gproto):
     segs, width = gview.shape[0] // 2, gview.shape[1]
     half = jax.ShapeDtypeStruct((segs, width), F32)
-    parts = 2 + gproto.shape[0] // segs
+    size = segs // 2
+    parts = (2 * segs + gproto.shape[0]) // size
     hbm = pl.BlockSpec(memory_space=pltpu.HBM)
     return pl.pallas_call(
         hand_over_kernel,
         out_shape=(half, half, jax.ShapeDtypeStruct(gproto.shape, F32)),
         in_specs=[hbm] * 2,
         out_specs=(hbm,) * 3,
-        scratch_shapes=[pltpu.VMEM((parts, segs, width), F32), pltpu.SemaphoreType.DMA((2, parts))],
+        scratch_shapes=[pltpu.VMEM((parts, size, width), F32), pltpu.SemaphoreType.DMA((2, parts))],
         compiler_params=pltpu.CompilerParams(vmem_limit_bytes=62 << 20),
         name="hand_over",
     )(gview, gproto)

time: 147 us -> 134 us (0.912)
  Pallas kernels: 146 us -> 132 us
    pallas_call x1, Pallas kernels: 138 us -> 123 us  [balance(): pl.pallas_call(functools.partial(balance_kernel, nx, ny, nz), out_shape=(...]
where the time goes in v5:
time: 134 us; the launch traced here: 133 us
  Pallas kernels  132 us (99%)
    pallas_call x1, Pallas kernels, balance(): pl.pallas_call(functools.partial(balance_kernel, nx, ny, nz), out_shape=(...  123 us
    pallas_call x1, Pallas kernels, hand_over(): pl.pallas_call(hand_over_kernel, out_shape=(half, half, jax.ShapeDtypeStr...  9.38 us

profile of v5, /device:TPU:1, one launch (start us, length us, event | category | flops | bytes accessed | tf_op | source)
XLA Modules:
  0.0 133.3 jit_solution(14174664518158459801)
XLA Ops:
  0.6 123.1 %balance.1 = (f32[1024,512]{1,0:T(8,128)}, f32[4096,512]{1,0:T(8,128)}) custom-call(bf16[512,512]{1,0:T(8,128)(2,1)} %one_hbm.1, bf16[512,512]{1,0:T(8,128)(2,1)} %two_hbm.1, bf16[4096,512]{1,0:T(8,128)(2,1)} %proto_hbm.1, s32[1,512]{1,0:T(1,128)} %pair_ref.1), custom_call_target="tpu_custom_call" | custom-call | tf_op jit(solution)/shard_map/balance/pallas_call | solution.py:525
  123.7 9.4 %hand_over.1 = (f32[512,512]{1,0:T(8,128)}, f32[512,512]{1,0:T(8,128)}, f32[4096,512]{1,0:T(8,128)}) custom-call(f32[1024,512]{1,0:T(8,128)} %get-tuple-element.5.gview, f32[4096,512]{1,0:T(8,128)} %get-tuple-element.6.gproto), custom_call_target="tpu_custom_call" | custom-call | tf_op jit(solution)/shard_map/hand_over/pallas_call | solution.py:606

commit v6 on v5

--- a/solution.py
+++ b/solution.py
@@ -58,10 +58,10 @@
 def balance_kernel(
     nx, ny, nz,
     one_hbm, two_hbm, proto_hbm, pair_ref,
-    gview_hbm, gproto_hbm,
-    raw, expo, dscore, low_seg, low_seg_t, low_two, low_proto, onehot, row_scale, prob_scale,
-    cols, cols_in, plane_in, weight, rows, rows_in, tile_u, row_part, tot_part,
-    dproto, from_core, dunit, own_proto, gproto, gview,
+    gview_hbm, gproto_hbm, pair_out,
+    raw, expo, dscore, low_seg, low_seg_t, low_proto, row_scale, prob_scale,
+    cols, cols_in, plane_in, weight, rows, rows_in, tile_u,
+    dproto, from_core, own_proto, gproto,
     a_relay, a_plain, a_joint, b_relay, b_plain, b_joint, z_relay, z_plain, z_joint,
     send_sem, recv_sem, local_sem,
 ):
@@ -93,7 +93,7 @@
     piece = protos // pieces
     fetch = [
         pltpu.make_async_copy(one_hbm, raw.at[0:segs], local_sem.at[0]),
-        pltpu.make_async_copy(two_hbm, raw.at[segs:both], local_sem.at[1]),
+        pltpu.make_async_copy(two_hbm, low_seg.at[0:segs], local_sem.at[1]),
         pltpu.make_async_copy(proto_hbm.at[pl.ds(mine * 128, 128)], own_proto, local_sem.at[2]),
     ]
     fetch_protos = [
@@ -121,16 +121,18 @@
     def norm_views(i, carry):
         at = pl.ds(pl.multiple_of(i * 128, 128), 128)
         low_seg[at, :] = unit(raw[at, :])
-        low_two[at, :] = unit(raw[pl.ds(pl.multiple_of(segs + i * 128, 128), 128), :])
         return carry
 
     fetch[0].wait()
     fetch[1].wait()
-    lax.fori_loop(0, segs // 128, norm_views, 0, unroll=2)
+    pair_out[...] = pair_ref[...]
     pair = jnp.broadcast_to(pair_ref[...], (segs, segs))
     number = lax.broadcasted_iota(jnp.int32, (segs, segs), 0)
+    onehot = dscore[0].at[0:segs]
     onehot[...] = jnp.where(pair == number, 1.0, 0.0).astype(BF16)
-    low_seg[segs:both, :] = dot(onehot[...], low_two[...], TN).astype(BF16)
+    raw[segs:both, :] = dot(onehot[...], low_seg[0:segs, :], TN).astype(BF16)
+    lax.fori_loop(0, both // 128, norm_views, 0, unroll=2)
+
     def norm_protos(i, carry):
         at = pl.ds(pl.multiple_of(i * 128, 128), 128)
         low_proto[at, :] = unit(low_proto[at, :])
@@ -212,6 +214,8 @@
         weight[it, tiles_of(core)] = 1.0 / total
         return links.send(weight.at[it, tiles_of(core)], weight.at[it, tiles_of(core)], sibling)
 
+    spare = dproto[7]
+
     def row_sums(it, with_total, view):
         def block(b, carry):
             at = pl.ds(pl.multiple_of(view * segs + b * 64, 64), 64)
@@ -225,19 +229,20 @@
                 acc = acc + (e * e) * v
                 if with_total:
                     tot = tot + e
-            row_part[at, :] = acc
+            spare[view, pl.ds(pl.multiple_of(b * 64, 64), 64), :] = acc
             if with_total:
-                tot_part[at, :] = tot
+                spare[2 + view, pl.ds(pl.multiple_of(b * 64, 64), 64), :] = tot
             return carry
 
         lax.fori_loop(0, segs // 64, block, 0)
 
     def turn_sums(it, with_total):
         for b in range(both // 128):
-            at = slice(b * 128, (b + 1) * 128)
-            rows[it, b:b + 1, :] = jnp.sum(jnp.transpose(row_part[at, :]), axis=0, keepdims=True)
+            view, at = b // 4, slice(b % 4 * 128, (b % 4 + 1) * 128)
+            rows[it, b:b + 1, :] = jnp.sum(jnp.transpose(spare[view, at, :]), axis=0, keepdims=True)
             if with_total:
-                rows[it, 8 + b:9 + b, :] = jnp.sum(jnp.transpose(tot_part[at, :]), axis=0, keepdims=True)
+                tot = jnp.sum(jnp.transpose(spare[2 + view, at, :]), axis=0, keepdims=True)
+                rows[it, 8 + b:9 + b, :] = tot
 
     def spread(out, row):
         for b in range(both // 128):
@@ -341,8 +346,13 @@
             plains[1] = links.send(low, a_plain.at[1], a_peer(3))
     d_right, d_left, d_own = dproto[3], dproto[5], dproto[7]
 
-    def views(i):
-        at = slice(i * 256, (i + 1) * 256)
+    dunit = expo.at[:, 0:width]
+    seg_part = both // nz
+    z_half = seg_part // 2
+    z_right, z_left, z_far = lax.rem(z + 1, 4), lax.rem(z + 3, 4), lax.rem(z + 2, 4)
+
+    def views(k):
+        at = pl.ds(pl.multiple_of(k * seg_part, seg_part), seg_part)
         total = None
         for g in range(8):
             rows_g = low_proto[pl.ds(pl.multiple_of(chunks[g] * 128, 512), 512), :]
@@ -350,8 +360,17 @@
             total = term if total is None else total + term
         dunit[at, :] = total
 
-    views(0)
-    views(1)
+    def part(ref, k, lower):
+        start = k * seg_part + (0 if lower else z_half)
+        return ref.at[pl.ds(pl.multiple_of(start, z_half), z_half)]
+
+    views(z_far)
+    z_relays = [
+        links.send(part(dunit, z_far, True), z_relay.at[0], z_peer(1)),
+        links.send(part(dunit, z_far, False), z_relay.at[1], z_peer(3)),
+    ]
+    views(z_right)
+    z_plains = [links.send(part(dunit, z_right, False), z_plain.at[0], z_peer(1))]
     relays[0].wait_recv()
     for q in range(2):
         d_right[q] = d_right[q] + a_relay[0, q]
@@ -361,31 +380,9 @@
         d_left[2 + q] = d_left[2 + q] + a_relay[1, q]
     joints[1] = links.send(d_left.at[2:4], a_joint.at[1], a_peer(3))
 
-    views(2)
-    views(3)
-    d = dunit[segs:both, :]
-    top = d.astype(BF16)
-    rest = d - top.astype(F32)
-    middle = rest.astype(BF16)
-    end = (rest - middle.astype(F32)).astype(BF16)
-    rest = dot(onehot[...], middle, NN) + dot(onehot[...], end, NN)
-    dunit[segs:both, :] = dot(onehot[...], top, NN) + rest
-
-    def part(ref, k, size, lower):
-        half = size // 2
-        start = k * size + (0 if lower else half)
-        return ref.at[pl.ds(pl.multiple_of(start, half), half)]
-
-    seg_part = both // nz
-    z_right, z_left, z_far = lax.rem(z + 1, 4), lax.rem(z + 3, 4), lax.rem(z + 2, 4)
-    z_relays = [
-        links.send(part(dunit, z_far, seg_part, True), z_relay.at[0], z_peer(1)),
-        links.send(part(dunit, z_far, seg_part, False), z_relay.at[1], z_peer(3)),
-    ]
-    z_plains = [
-        links.send(part(dunit, z_right, seg_part, False), z_plain.at[0], z_peer(1)),
-        links.send(part(dunit, z_left, seg_part, True), z_plain.at[1], z_peer(3)),
-    ]
+    views(z_left)
+    z_plains.append(links.send(part(dunit, z_left, True), z_plain.at[1], z_peer(3)))
+    views(z)
 
     for copy in plains + joints:
         copy.wait_recv()
@@ -403,7 +400,6 @@
         links.send(d_own.at[b_left, 0:width_half], b_plain.at[1], b_peer(3)),
     ]
 
-    z_half = seg_part // 2
     z_joints = []
     for way, k, skip, peer in ((0, z_right, 0, z_peer(1)), (1, z_left, z_half, z_peer(3))):
         z_relays[way].wait_recv()
@@ -451,8 +447,8 @@
     at = pl.ds(pl.multiple_of(z * seg_part + z_half, z_half), z_half)
     dunit[at, :] = dunit[at, :] + (z_plain[0] + z_joint[1])
     at = pl.ds(pl.multiple_of(z * seg_part, seg_part), seg_part)
-    gview[...] = back(dunit[at, :], raw[at, :])
-    place = gview_hbm.at[at]
+    dunit[at, :] = back(dunit[at, :], raw[at, :])
+    gview, place = dunit.at[at], gview_hbm.at[at]
     z_whole = [links.send(gview, place, z_peer(1)), links.send(gview, place, z_peer(3))]
     keep_view = pltpu.make_async_copy(gview, place, local_sem.at[12])
     keep_view.start()
@@ -521,24 +517,23 @@
     both = 2 * segs
     z_half = both // nz // 2
     copies = ITERS * (nx * ny + nz + 1) + 80
-    hbm = pl.BlockSpec(memory_space=pl.ANY)
+    vmem, hbm = pl.BlockSpec(memory_space=pltpu.VMEM), pl.BlockSpec(memory_space=pl.ANY)
     return pl.pallas_call(
         functools.partial(balance_kernel, nx, ny, nz),
         out_shape=(
-            jax.ShapeDtypeStruct((both, width), F32),
-            jax.ShapeDtypeStruct((count, width), F32),
+            pltpu.VMEM((both, width), F32),
+            pltpu.VMEM((count, width), F32),
+            pltpu.VMEM(pair.shape, jnp.int32),
         ),
-        in_specs=[hbm, hbm, hbm, pl.BlockSpec(memory_space=pltpu.VMEM)],
-        out_specs=(hbm, hbm),
+        in_specs=[hbm, hbm, hbm, vmem],
+        out_specs=(hbm, hbm, vmem),
         scratch_shapes=[
             pltpu.VMEM((both, width), BF16),
             pltpu.VMEM((both, count), F32),
             [pltpu.VMEM((both, count // 8), BF16)] * 8,
             pltpu.VMEM((both, width), BF16),
             pltpu.VMEM((width, both), BF16),
-            pltpu.VMEM((segs, width), BF16),
             pltpu.VMEM((count, width), BF16),
-            pltpu.VMEM((segs, segs), BF16),
             pltpu.VMEM((both, 128), F32),
             pltpu.VMEM((both, 128), F32),
             pltpu.VMEM((ITERS, 8, 8, 128), F32),
@@ -548,14 +543,10 @@
             pltpu.VMEM((ITERS, 16, 128), F32),
             pltpu.VMEM((ITERS, nz, 16, 128), F32),
             pltpu.VMEM((16, 128), F32),
-            pltpu.VMEM((both, 128), F32),
-            pltpu.VMEM((both, 128), F32),
             [pltpu.VMEM((4, width, 128), F32)] * 8,
             pltpu.VMEM((4, 4, width, 128), F32),
-            pltpu.VMEM((both, width), F32),
             pltpu.VMEM((128, width), BF16),
             pltpu.VMEM((128, width), F32),
-            pltpu.VMEM((both // nz, width), F32),
         ]
         + [pltpu.VMEM((2, 2, width, 128), F32)] * 3
         + [pltpu.VMEM((2, width // 2, 128), F32)] * 3
@@ -566,57 +557,57 @@
             pltpu.SemaphoreType.DMA((13,)),
         ],
         compiler_params=pltpu.CompilerParams(
-            collective_id=0, has_side_effects=True, vmem_limit_bytes=62 << 20
+            collective_id=0, has_side_effects=True, vmem_limit_bytes=53 << 20
         ),
         name="balance",
     )(one, two, protos, pair)
 
 
-def hand_over_kernel(gview, gproto, one_out, two_out, proto_out, stage, sems):
-    size = stage.shape[1]
-    pairs = []
-    for i in range(one_out.shape[0] // size):
+def hand_over_kernel(gview, gproto, pair_ref, one_out, two_out, proto_out, two, sems):
+    segs = one_out.shape[0]
+    parts = 8
+    size = proto_out.shape[0] // parts
+    copies = [pltpu.make_async_copy(gview.at[0:segs], one_out, sems.at[parts])]
+    for i in range(parts):
         at = slice(i * size, (i + 1) * size)
-        pairs.append((gview.at[at], one_out.at[at]))
-        late = slice(one_out.shape[0] + i * size, one_out.shape[0] + (i + 1) * size)
-        pairs.append((gview.at[late], two_out.at[at]))
-    for i in range(proto_out.shape[0] // size):
-        at = slice(i * size, (i + 1) * size)
-        pairs.append((gproto.at[at], proto_out.at[at]))
-    come = [pltpu.make_async_copy(src, stage.at[i], sems.at[0, i]) for i, (src, _) in enumerate(pairs)]
-    go = [pltpu.make_async_copy(stage.at[i], dst, sems.at[1, i]) for i, (_, dst) in enumerate(pairs)]
-    ahead = 4
-    for copy in come[:ahead]:
+        copies.append(pltpu.make_async_copy(gproto.at[at], proto_out.at[at], sems.at[i]))
+    for copy in copies:
         copy.start()
-    for i, copy in enumerate(go):
-        come[i].wait()
-        copy.start()
-        if i + ahead < len(come):
-            come[i + ahead].start()
-    for copy in go:
+    pair = jnp.broadcast_to(pair_ref[...], (segs, segs))
+    number = lax.broadcasted_iota(jnp.int32, (segs, segs), 0)
+    onehot = jnp.where(pair == number, 1.0, 0.0).astype(BF16)
+    d = gview[segs:2 * segs, :]
+    top = d.astype(BF16)
+    rest = d - top.astype(F32)
+    middle = rest.astype(BF16)
+    end = (rest - middle.astype(F32)).astype(BF16)
+    two[...] = dot(onehot, top, NN) + (dot(onehot, middle, NN) + dot(onehot, end, NN))
+    copies.append(pltpu.make_async_copy(two, two_out, sems.at[parts + 1]))
+    copies[-1].start()
+    for copy in copies:
         copy.wait()
 
 
-def hand_over(gview, gproto):
+def hand_over(gview, gproto, pairing):
     segs, width = gview.shape[0] // 2, gview.shape[1]
     half = jax.ShapeDtypeStruct((segs, width), F32)
-    size = segs // 2
-    parts = (2 * segs + gproto.shape[0]) // size
-    hbm = pl.BlockSpec(memory_space=pltpu.HBM)
+    vmem, hbm = pl.BlockSpec(memory_space=pltpu.VMEM), pl.BlockSpec(memory_space=pl.ANY)
     return pl.pallas_call(
         hand_over_kernel,
         out_shape=(half, half, jax.ShapeDtypeStruct(gproto.shape, F32)),
-        in_specs=[hbm] * 2,
+        in_specs=[vmem, hbm, vmem],
         out_specs=(hbm,) * 3,
-        scratch_shapes=[pltpu.VMEM((parts, size, width), F32), pltpu.SemaphoreType.DMA((2, parts))],
-        compiler_params=pltpu.CompilerParams(vmem_limit_bytes=62 << 20),
+        scratch_shapes=[
+            pltpu.VMEM((segs, width), F32),
+            pltpu.SemaphoreType.DMA((10,)),
+        ],
+        compiler_params=pltpu.CompilerParams(vmem_limit_bytes=10 << 20),
         name="hand_over",
-    )(gview, gproto)
+    )(gview, gproto, pairing)
 
 
 def per_device(mesh, view_one, view_two, prototypes, pairing):
-    gview, gproto = balance(mesh, view_one, view_two, prototypes, pairing)
-    return hand_over(gview, gproto)
+    return hand_over(*balance(mesh, view_one, view_two, prototypes, pairing))
 
 
 def solution(mesh):

time: 134 us -> 128 us (0.955)
  Pallas kernels: 132 us -> 127 us
    pallas_call x1, Pallas kernels: 9.38 us -> 4.02 us  [hand_over(): pl.pallas_call(hand_over_kernel, out_shape=(half, half, jax.ShapeDtypeStr...]
where the time goes in v6:
time: 128 us
  Pallas kernels  127 us (99%)
    pallas_call x1, Pallas kernels, balance(): pl.pallas_call(functools.partial(balance_kernel, nx, ny, nz), out_shape=(...  123 us
    pallas_call x1, Pallas kernels, hand_over(): pl.pallas_call(hand_over_kernel, out_shape=(half, half, jax.ShapeDtypeStr...  4.02 us

profile of v6, /device:TPU:1, one launch (start us, length us, event | category | flops | bytes accessed | tf_op | source)
XLA Modules:
  0.0 128.1 jit_solution(5661514991255730535)
XLA Ops:
  0.6 123.3 %balance.1 = (f32[1024,512]{1,0:T(8,128)S(1)}, f32[4096,512]{1,0:T(8,128)S(1)}, s32[1,512]{1,0:T(1,128)S(1)}) custom-call(bf16[512,512]{1,0:T(8,128)(2,1)} %one_hbm.1, bf16[512,512]{1,0:T(8,128)(2,1)} %two_hbm.1, bf16[4096,512]{1,0:T(8,128)(2,1)} %proto_hbm.1, s32[1,512]{1,0:T(1,128)} %pair_ref.1), custom_call_target="tpu_custom_call" | custom-call | tf_op jit(solution)/shard_map/balance/pallas_call | solution.py:521
  123.9 4.0 %hand_over.1 = (f32[512,512]{1,0:T(8,128)}, f32[512,512]{1,0:T(8,128)}, f32[4096,512]{1,0:T(8,128)}) custom-call(f32[1024,512]{1,0:T(8,128)S(1)} %get-tuple-element.6.gview, f32[4096,512]{1,0:T(8,128)S(1)} %get-tuple-element.7.gproto, s32[1,512]{1,0:T(1,128)S(1)} %get-tuple-element.8.pair_ref), custom_call_target="tpu_custom_call" | custom-call | tf_op jit(solution)/shard_map/hand_over/pallas_call | solution.py:595

commit v7 on v6

--- a/solution.py
+++ b/solution.py
@@ -311,8 +311,9 @@
             if old is not None:
                 at = pl.ds(pl.multiple_of(j * half_b, half_b), half_b)
                 part = dot(low_seg_t[...], dscore[old][:, at], NN)
-                dproto[old][2 * j] = part[:, 0:128]
-                dproto[old][2 * j + 1] = part[:, 128:256]
+                middle = at_a if old % 2 == 0 else at_b
+                dproto[old][lax.rem(2 * j + 6 - middle, 4)] = part[:, 0:128]
+                dproto[old][lax.rem(2 * j + 7 - middle, 4)] = part[:, 128:256]
             if new is not None:
                 elements(dscore[new], chunks[new], j)
             return carry
@@ -325,7 +326,7 @@
         for half, place in ((1 - core, at_b), (core, at_a)):
             spots.append(lax.rem(place + t, 4))
             chunks.append(half * 16 + spots[-1] * 4)
-    relays, plains, joints = [None] * 2, [None] * 2, [None] * 2
+    relays, plains = [None] * 2, [None] * 2
     crossing = [None] * 8
     step(0, None)
     for g in range(8):
@@ -372,33 +373,37 @@
     views(z_right)
     z_plains = [links.send(part(dunit, z_right, False), z_plain.at[0], z_peer(1))]
     relays[0].wait_recv()
-    for q in range(2):
+    low_joints, high_joints = [None] * 2, [None] * 2
+    for q in (0, 1):
         d_right[q] = d_right[q] + a_relay[0, q]
-    joints[0] = links.send(d_right.at[0:2], a_joint.at[0], a_peer(1))
+        low_joints[q] = links.send(d_right.at[q], a_joint.at[0, q], a_peer(1))
     relays[1].wait_recv()
-    for q in range(2):
+    for q in (1, 0):
         d_left[2 + q] = d_left[2 + q] + a_relay[1, q]
-    joints[1] = links.send(d_left.at[2:4], a_joint.at[1], a_peer(3))
+        high_joints[q] = links.send(d_left.at[2 + q], a_joint.at[1, q], a_peer(3))
 
     views(z_left)
     z_plains.append(links.send(part(dunit, z_left, True), z_plain.at[1], z_peer(3)))
     views(z)
 
-    for copy in plains + joints:
+    far, left, right = 0, 1, 3
+    width_half = width // 2
+    for copy in plains:
         copy.wait_recv()
-    for q in range(2):
-        d_own[q] = d_own[q] + (a_joint[0, q] + a_plain[1, q])
-        d_own[2 + q] = d_own[2 + q] + (a_plain[0, q] + a_joint[1, q])
-    b_right, b_left, b_far = lax.rem(at_b + 1, 4), lax.rem(at_b + 3, 4), lax.rem(at_b + 2, 4)
-    width_half = width // 2
+    low_joints[0].wait_recv()
+    d_own[far] = d_own[far] + (a_joint[0, 0] + a_plain[1, 0])
     b_relays = [
-        links.send(d_own.at[b_far, 0:width_half], b_relay.at[0], b_peer(1)),
-        links.send(d_own.at[b_far, width_half:width], b_relay.at[1], b_peer(3)),
+        links.send(d_own.at[far, 0:width_half], b_relay.at[0], b_peer(1)),
+        links.send(d_own.at[far, width_half:width], b_relay.at[1], b_peer(3)),
     ]
-    b_plains = [
-        links.send(d_own.at[b_right, width_half:width], b_plain.at[0], b_peer(1)),
-        links.send(d_own.at[b_left, 0:width_half], b_plain.at[1], b_peer(3)),
-    ]
+    high_joints[1].wait_recv()
+    d_own[right] = d_own[right] + (a_plain[0, 1] + a_joint[1, 1])
+    b_plains = [links.send(d_own.at[right, width_half:width], b_plain.at[0], b_peer(1))]
+    low_joints[1].wait_recv()
+    d_own[left] = d_own[left] + (a_joint[0, 1] + a_plain[1, 1])
+    b_plains.append(links.send(d_own.at[left, 0:width_half], b_plain.at[1], b_peer(3)))
+    high_joints[0].wait_recv()
+    d_own[2] = d_own[2] + (a_plain[0, 0] + a_joint[1, 0])
 
     z_joints = []
     for way, k, skip, peer in ((0, z_right, 0, z_peer(1)), (1, z_left, z_half, z_peer(3))):
@@ -408,14 +413,14 @@
         z_joints.append(links.send(dunit.at[at], z_joint.at[way], peer))
 
     b_joints = []
-    for way, k, skip, peer in ((0, b_right, 0, b_peer(1)), (1, b_left, width_half, b_peer(3))):
+    for way, k, skip, peer in ((0, right, 0, b_peer(1)), (1, left, width_half, b_peer(3))):
         b_relays[way].wait_recv()
         at = slice(skip, skip + width_half)
         d_own[k, at, :] = d_own[k, at, :] + b_relay[way]
         b_joints.append(links.send(d_own.at[k, at], b_joint.at[way], peer))
     for copy in b_plains + b_joints:
         copy.wait_recv()
-    me = at_b
+    me = 2
     d_own[me, 0:width_half, :] = d_own[me, 0:width_half, :] + (b_joint[0] + b_plain[1])
     d_own[me, width_half:width, :] = d_own[me, width_half:width, :] + (b_plain[0] + b_joint[1])
     fetch[2].wait()
@@ -434,8 +439,23 @@
     def to_sibling(place, src=None):
         across.append(links.send(place if src is None else src, place, sibling))
 
-    b_whole = [links.send(gproto, rows_of(mine), b_peer(1)), links.send(gproto, rows_of(mine), b_peer(3))]
-    a_whole = {0: [links.send(gproto, rows_of(mine), a_peer(1)), links.send(gproto, rows_of(mine), a_peer(3))]}
+    b_right, b_left, b_far = lax.rem(at_b + 1, 4), lax.rem(at_b + 3, 4), lax.rem(at_b + 2, 4)
+    a_right, a_left, a_far = lax.rem(at_a + 1, 4), lax.rem(at_a + 3, 4), lax.rem(at_a + 2, 4)
+    b_in, a_in, a_halves = {}, {}, {}
+
+    def along_a(key, b, part, src=None):
+        place = rows_of(chunk_of(at_a, b), part)
+        src = place if src is None else src
+        a_in[key, 0, part] = links.send(src, place, a_peer(1))
+        a_in[key, 1, part] = links.send(src, place, a_peer(3))
+
+    mine_half = [gproto.at[0:64], gproto.at[64:128]]
+    b_in[0, 0] = links.send(mine_half[0], rows_of(mine, 0), b_peer(1))
+    b_in[1, 1] = links.send(mine_half[1], rows_of(mine, 1), b_peer(3))
+    along_a(0, at_b, 0, mine_half[0])
+    b_in[0, 1] = links.send(mine_half[1], rows_of(mine, 1), b_peer(1))
+    b_in[1, 0] = links.send(mine_half[0], rows_of(mine, 0), b_peer(3))
+    along_a(0, at_b, 1, mine_half[1])
     to_sibling(rows_of(mine), gproto)
     keep = pltpu.make_async_copy(gproto, rows_of(mine), local_sem.at[11])
     keep.start()
@@ -453,34 +473,40 @@
     keep_view = pltpu.make_async_copy(gview, place, local_sem.at[12])
     keep_view.start()
 
-    b_halves, a_halves = [], {}
-    a_right, a_left, a_far = lax.rem(at_a + 1, 4), lax.rem(at_a + 3, 4), lax.rem(at_a + 2, 4)
-
-    def along_a(key, place):
-        a_whole[key] = a_whole.get(key, []) + [links.send(place, place, a_peer(1)), links.send(place, place, a_peer(3))]
-        to_sibling(place)
-
-    b_whole[0].wait_recv()
-    b_halves.append(links.send(rows_of(chunk_of(at_a, b_left), 0), rows_of(chunk_of(at_a, b_left), 0), b_peer(1)))
-    along_a(3, rows_of(chunk_of(at_a, b_left)))
-    b_whole[1].wait_recv()
-    b_halves.append(links.send(rows_of(chunk_of(at_a, b_right), 1), rows_of(chunk_of(at_a, b_right), 1), b_peer(3)))
-    along_a(1, rows_of(chunk_of(at_a, b_right)))
+    b_in[0, 0].wait_recv()
+    from_left, from_right = chunk_of(at_a, b_left), chunk_of(at_a, b_right)
+    b_halves = [links.send(rows_of(from_left, 0), rows_of(from_left, 0), b_peer(1))]
+    along_a(3, b_left, 0)
+    b_in[1, 1].wait_recv()
+    b_halves.append(links.send(rows_of(from_right, 1), rows_of(from_right, 1), b_peer(3)))
+    along_a(1, b_right, 1)
+    b_in[0, 1].wait_recv()
+    along_a(3, b_left, 1)
+    b_in[1, 0].wait_recv()
+    along_a(1, b_right, 0)
+    to_sibling(rows_of(from_left))
+    to_sibling(rows_of(from_right))
 
     def pass_on(key, b):
         left, right = chunk_of(a_left, b), chunk_of(a_right, b)
-        a_whole[key][0].wait_recv()
+        a_in[key, 0, 0].wait_recv()
         a_halves[key] = [links.send(rows_of(left, 0), rows_of(left, 0), a_peer(1))]
-        to_sibling(rows_of(left))
-        a_whole[key][1].wait_recv()
+        a_in[key, 1, 1].wait_recv()
         a_halves[key].append(links.send(rows_of(right, 1), rows_of(right, 1), a_peer(3)))
-        to_sibling(rows_of(right))
+
+    def settle(key, b):
+        a_in[key, 0, 1].wait_recv()
+        to_sibling(rows_of(chunk_of(a_left, b)))
+        a_in[key, 1, 0].wait_recv()
+        to_sibling(rows_of(chunk_of(a_right, b)))
 
     pass_on(0, at_b)
-    far = chunk_of(at_a, b_far)
     b_halves[0].wait_recv()
+    along_a(2, b_far, 0)
     b_halves[1].wait_recv()
-    along_a(2, rows_of(far))
+    along_a(2, b_far, 1)
+    to_sibling(rows_of(chunk_of(at_a, b_far)))
+    settle(0, at_b)
 
     z_left_place = gview_hbm.at[pl.ds(pl.multiple_of(z_left * seg_part, seg_part), z_half)]
     z_right_place = gview_hbm.at[pl.ds(pl.multiple_of(z_right * seg_part + z_half, z_half), z_half)]
@@ -491,6 +517,8 @@
 
     pass_on(3, b_left)
     pass_on(1, b_right)
+    settle(3, b_left)
+    settle(1, b_right)
 
     def far_halves(key, b):
         chunk = chunk_of(a_far, b)
@@ -502,6 +530,7 @@
     pass_on(2, b_far)
     far_halves(3, b_left)
     far_halves(1, b_right)
+    settle(2, b_far)
     far_halves(2, b_far)
     for copy in z_halves + across:
         copy.wait_recv()
@@ -516,7 +545,7 @@
     count = protos.shape[0]
     both = 2 * segs
     z_half = both // nz // 2
-    copies = ITERS * (nx * ny + nz + 1) + 80
+    copies = ITERS * (nx * ny + nz + 1) + 100
     vmem, hbm = pl.BlockSpec(memory_space=pltpu.VMEM), pl.BlockSpec(memory_space=pl.ANY)
     return pl.pallas_call(
         functools.partial(balance_kernel, nx, ny, nz),

time: 128 us -> 124 us (0.969)
  Pallas kernels: 127 us -> 123 us
    pallas_call x1, Pallas kernels: 123 us -> 119 us  [balance(): pl.pallas_call(functools.partial(balance_kernel, nx, ny, nz), out_shape=(...]
where the time goes in v7:
time: 124 us
  Pallas kernels  123 us (99%)
    pallas_call x1, Pallas kernels, balance(): pl.pallas_call(functools.partial(balance_kernel, nx, ny, nz), out_shape=(...  119 us
    pallas_call x1, Pallas kernels, hand_over(): pl.pallas_call(hand_over_kernel, out_shape=(half, half, jax.ShapeDtypeStr...  4.02 us

profile of v7, /device:TPU:1, one launch (start us, length us, event | category | flops | bytes accessed | tf_op | source)
XLA Modules:
  0.0 123.7 jit_solution(2676299620795544671)
XLA Ops:
  0.6 118.9 %balance.1 = (f32[1024,512]{1,0:T(8,128)S(1)}, f32[4096,512]{1,0:T(8,128)S(1)}, s32[1,512]{1,0:T(1,128)S(1)}) custom-call(bf16[512,512]{1,0:T(8,128)(2,1)} %one_hbm.1, bf16[512,512]{1,0:T(8,128)(2,1)} %two_hbm.1, bf16[4096,512]{1,0:T(8,128)(2,1)} %proto_hbm.1, s32[1,512]{1,0:T(1,128)} %pair_ref.1), custom_call_target="tpu_custom_call" | custom-call | tf_op jit(solution)/shard_map/balance/pallas_call | solution.py:550
  119.5 4.0 %hand_over.1 = (f32[512,512]{1,0:T(8,128)}, f32[512,512]{1,0:T(8,128)}, f32[4096,512]{1,0:T(8,128)}) custom-call(f32[1024,512]{1,0:T(8,128)S(1)} %get-tuple-element.6.gview, f32[4096,512]{1,0:T(8,128)S(1)} %get-tuple-element.7.gproto, s32[1,512]{1,0:T(1,128)S(1)} %get-tuple-element.8.pair_ref), custom_call_target="tpu_custom_call" | custom-call | tf_op jit(solution)/shard_map/hand_over/pallas_call | solution.py:624

commit v8 on v7

--- a/solution.py
+++ b/solution.py
@@ -144,20 +144,23 @@
 
     wide = protos // 4
 
-    def scores(j, carry):
-        for q in range(wide // 256):
-            at = pl.ds(pl.multiple_of(j * wide + q * 256, 256), 256)
-            s = dot(low_seg[...], low_proto[at, :], NT)
-            e = jnp.exp2(s * (10.0 * LOG2E))
-            expo[:, at] = e
-            k = e * e
-            for view in range(2):
-                total = jnp.sum(k[view * segs:(view + 1) * segs], axis=0, keepdims=True)
+    def scores(view):
+        ours = pl.ds(pl.multiple_of(view * segs, segs), segs)
+
+        def block(j, carry):
+            for q in range(wide // 256):
+                at = pl.ds(pl.multiple_of(j * wide + q * 256, 256), 256)
+                s = dot(low_seg[ours, :], low_proto[at, :], NT)
+                e = jnp.exp2(s * (10.0 * LOG2E))
+                expo[ours, at] = e
+                total = jnp.sum(e * e, axis=0, keepdims=True)
                 for h in range(2):
                     cols[0, view * 4 + j, q * 2 + h:q * 2 + h + 1, :] = total[:, h * 128:(h + 1) * 128]
-        return carry
-
-    lax.fori_loop(0, 4, scores, 0)
+            return carry
+
+        lax.fori_loop(0, 4, block, 0)
+
+    scores(1 - core)
 
     def col_sums(it, view):
         def block(j, carry):
@@ -253,7 +256,7 @@
         size = 16 if with_total else 8
         rows_in[it, z] = rows[it]
         copies = []
-        for s in range(1, nz):
+        for s in (2, 1, 3):
             copies.append(links.send(rows.at[it, 0:size], rows_in.at[it, z, 0:size], z_peer(s)))
         for copy in copies:
             copy.wait_recv()
@@ -274,6 +277,7 @@
             col_sums(it, core)
         else:
             swap = swap_cols(it)
+            scores(core)
         back_copy = all_cols(it, swap)
         row_sums(it, it == 0, core)
         back_copy.wait_recv()

time: 124 us -> 123 us (level)
  no operation moved by 1% of the time
where the time goes in v8:
time: 123 us
  Pallas kernels  122 us (99%)
    pallas_call x1, Pallas kernels, balance(): pl.pallas_call(functools.partial(balance_kernel, nx, ny, nz), out_shape=(...  118 us
    pallas_call x1, Pallas kernels, hand_over(): pl.pallas_call(hand_over_kernel, out_shape=(half, half, jax.ShapeDtypeStr...  4.02 us

profile of v8, /device:TPU:1, one launch (start us, length us, event | category | flops | bytes accessed | tf_op | source)
XLA Modules:
  0.0 123.3 jit_solution(9187377413674094938)
XLA Ops:
  0.6 118.4 %balance.1 = (f32[1024,512]{1,0:T(8,128)S(1)}, f32[4096,512]{1,0:T(8,128)S(1)}, s32[1,512]{1,0:T(1,128)S(1)}) custom-call(bf16[512,512]{1,0:T(8,128)(2,1)} %one_hbm.1, bf16[512,512]{1,0:T(8,128)(2,1)} %two_hbm.1, bf16[4096,512]{1,0:T(8,128)(2,1)} %proto_hbm.1, s32[1,512]{1,0:T(1,128)} %pair_ref.1), custom_call_target="tpu_custom_call" | custom-call | tf_op jit(solution)/shard_map/balance/pallas_call | solution.py:554
  119.1 4.0 %hand_over.1 = (f32[512,512]{1,0:T(8,128)}, f32[512,512]{1,0:T(8,128)}, f32[4096,512]{1,0:T(8,128)}) custom-call(f32[1024,512]{1,0:T(8,128)S(1)} %get-tuple-element.6.gview, f32[4096,512]{1,0:T(8,128)S(1)} %get-tuple-element.7.gproto, s32[1,512]{1,0:T(1,128)S(1)} %get-tuple-element.8.pair_ref), custom_call_target="tpu_custom_call" | custom-call | tf_op jit(solution)/shard_map/hand_over/pallas_call | solution.py:628

commit v9 on v8

--- a/solution.py
+++ b/solution.py
@@ -42,10 +42,10 @@
         self.sent.append(copy)
         return copy
 
-    def drain(self):
-        for copy in self.sent:
+    def drain(self, count):
+        for copy in self.sent[:count]:
             copy.wait_send()
-        self.sent = []
+        self.sent = self.sent[count:]
 
 
 def back(d, raw):
@@ -326,6 +326,7 @@
 
     order = (2, 1, 3, 0)
     chunks, spots = [], []
+    small_sends = len(links.sent)
     for t in order:
         for half, place in ((1 - core, at_b), (core, at_a)):
             spots.append(lax.rem(place + t, 4))
@@ -376,6 +377,7 @@
     ]
     views(z_right)
     z_plains = [links.send(part(dunit, z_right, False), z_plain.at[0], z_peer(1))]
+    links.drain(small_sends)
     relays[0].wait_recv()
     low_joints, high_joints = [None] * 2, [None] * 2
     for q in (0, 1):
@@ -446,6 +448,7 @@
     b_right, b_left, b_far = lax.rem(at_b + 1, 4), lax.rem(at_b + 3, 4), lax.rem(at_b + 2, 4)
     a_right, a_left, a_far = lax.rem(at_a + 1, 4), lax.rem(at_a + 3, 4), lax.rem(at_a + 2, 4)
     b_in, a_in, a_halves = {}, {}, {}
+    sum_sends = len(links.sent)
 
     def along_a(key, b, part, src=None):
         place = rows_of(chunk_of(at_a, b), part)
@@ -477,6 +480,7 @@
     keep_view = pltpu.make_async_copy(gview, place, local_sem.at[12])
     keep_view.start()
 
+    links.drain(sum_sends)
     b_in[0, 0].wait_recv()
     from_left, from_right = chunk_of(at_a, b_left), chunk_of(at_a, b_right)
     b_halves = [links.send(rows_of(from_left, 0), rows_of(from_left, 0), b_peer(1))]
@@ -540,7 +544,7 @@
         copy.wait_recv()
     keep.wait()
     keep_view.wait()
-    links.drain()
+    links.drain(len(links.sent))
 
 
 def balance(mesh, one, two, protos, pair):

time: 123 us -> 123 us (level)
  no operation moved by 1% of the time
where the time goes in v9:
time: 123 us
  Pallas kernels  122 us (99%)
    pallas_call x1, Pallas kernels, balance(): pl.pallas_call(functools.partial(balance_kernel, nx, ny, nz), out_shape=(...  118 us
    pallas_call x1, Pallas kernels, hand_over(): pl.pallas_call(hand_over_kernel, out_shape=(half, half, jax.ShapeDtypeStr...  4.02 us

profile of v9, /device:TPU:1, one launch (start us, length us, event | category | flops | bytes accessed | tf_op | source)
XLA Modules:
  0.0 123.2 jit_solution(15412254656375889750)
XLA Ops:
  0.6 118.4 %balance.1 = (f32[1024,512]{1,0:T(8,128)S(1)}, f32[4096,512]{1,0:T(8,128)S(1)}, s32[1,512]{1,0:T(1,128)S(1)}) custom-call(bf16[512,512]{1,0:T(8,128)(2,1)} %one_hbm.1, bf16[512,512]{1,0:T(8,128)(2,1)} %two_hbm.1, bf16[4096,512]{1,0:T(8,128)(2,1)} %proto_hbm.1, s32[1,512]{1,0:T(1,128)} %pair_ref.1), custom_call_target="tpu_custom_call" | custom-call | tf_op jit(solution)/shard_map/balance/pallas_call | solution.py:558
  119.0 4.0 %hand_over.1 = (f32[512,512]{1,0:T(8,128)}, f32[512,512]{1,0:T(8,128)}, f32[4096,512]{1,0:T(8,128)}) custom-call(f32[1024,512]{1,0:T(8,128)S(1)} %get-tuple-element.6.gview, f32[4096,512]{1,0:T(8,128)S(1)} %get-tuple-element.7.gproto, s32[1,512]{1,0:T(1,128)S(1)} %get-tuple-element.8.pair_ref), custom_call_target="tpu_custom_call" | custom-call | tf_op jit(solution)/shard_map/hand_over/pallas_call | solution.py:632
